TPU v7x, 128 devices: a whole 4x4x4 slice. The times are simulated.
128 devices in a mesh: row: 8 (over z_lo, x), col: 16 (over y, z_hi, core).
Axes of the slice: x: 4, y: 4, z: 4 (z_hi: 2, z_lo: 2; z = z_hi * 2 + z_lo), core: 2. Of those that a mesh axis runs over, the one named last changes fastest.
Arguments:
- pair_act: bfloat16 [512, 512, 128], P('row', 'col'), may hold values from -6 to 6
- out_grad: bfloat16 [512, 512, 128], P('row', 'col'), may hold values from -6 to 6
- tri_bias: bfloat16 [4, 512, 512], P(None, 'row', 'col'), may hold values from -6 to 250
- w_query: bfloat16 [128, 128], replicated, may hold values from -0.5 to 0.5
- w_key: bfloat16 [128, 128], replicated, may hold values from -0.5 to 0.5
- w_value: bfloat16 [128, 128], replicated, may hold values from -0.5 to 0.5
- w_gate: bfloat16 [128, 128], replicated, may hold values from -0.5 to 0.5
- w_out: bfloat16 [128, 128], replicated, may hold values from -0.5 to 0.5
- key_blocks: int32 [4, 3], replicated, may hold values from 0 to 3, as said below
- list_len: int32 [4], replicated, may hold values from 1 to 3, as said below
Outputs:
- d_pair: bfloat16 [512, 512, 128], P('row', 'col')
- d_bias: float32 [4, 512, 512], P(None, 'row', 'col')
- d_w_query: float32 [128, 128], replicated
- d_w_key: float32 [128, 128], replicated
- d_w_value: float32 [128, 128], replicated
- d_w_gate: float32 [128, 128], replicated
- d_w_out: float32 [128, 128], replicated
Inputs may be any that keep to these rules, and one draw needn't show every extreme that they name: `key_blocks`: entry 0 of query block b's list is b itself; its first list_len[b] entries are distinct; entries past list_len[b] are block numbers that must be ignored. `list_len`: some query block lists 3 key blocks.
All inputs are finite; a program needn't handle non-finite values.
Results may differ from a plain program's by a relative error of at most 0.015.
Values may be sent and summed in bfloat16 or wider, within the bound.
A program may use at most 128 MiB of HBM per device.

v0:
```python
import jax
import jax.numpy as jnp
from jax import lax
from jax.sharding import PartitionSpec as P


def in_one_piece(arrays, axis, split_dim, concat_dim, along):
    ends, at = ([], 0)
    for a in arrays[:-1]:
        at += a.shape[along]
        ends.append(at)
    both = jnp.concatenate(arrays, axis=along)
    return tuple(
        jnp.split(
            lax.all_to_all(both, axis, split_axis=split_dim, concat_axis=concat_dim, tiled=True),
            ends,
            axis=along,
        )
    )


def from_everyone(x, axis):
    devices = lax.axis_size(axis)
    return lax.all_to_all(jnp.broadcast_to(x[None], (devices, *x.shape)), axis, 0, 0, tiled=True)


def in_order(parts, dim):
    dims = list(parts.shape[1:])
    dims[dim] *= parts.shape[0]
    return jnp.moveaxis(parts, 0, dim).reshape(dims)


def gathered_copies(x, axis, dim):
    parts = from_everyone(x, axis)
    return in_order(parts, dim)


def cut_along(x, dim, devices):
    dims = x.shape
    parts = x.reshape(*dims[:dim], devices, dims[dim] // devices, *dims[dim + 1 :])
    return jnp.moveaxis(parts, dim, 0)


def summed_on_arrival(x, axis, dim):
    parts = cut_along(x, dim, lax.axis_size(axis))
    arrived = lax.all_to_all(parts, axis, split_axis=0, concat_axis=0, tiled=True)
    return arrived.astype(jnp.float32).sum(axis=0)


def on_device(
    pair_act, out_grad, tri_bias, w_query, w_key, w_value, w_gate, w_out, key_blocks, list_len
):
    row_count = lax.axis_size("row")
    tile_rows, tile_cols, chan_width = pair_act.shape
    head_count = tri_bias.shape[0]
    query_tile = tri_bias.shape[2]
    proj_width = w_query.shape[1]
    head_dim = proj_width // head_count
    block_count, slot_count = key_blocks.shape
    token_count = tile_rows * row_count
    block_size = token_count // block_count
    col_width = tile_cols // row_count
    score_scale = head_dim ** (-0.5)
    highest = lax.Precision.HIGHEST
    col_acts, col_grads = in_one_piece((pair_act, out_grad), "row", 1, 0, 2)
    spread = gathered_copies(tri_bias, "col", 2)
    bias_full = gathered_copies(spread, "row", 1)
    bias_blocks = bias_full.reshape(head_count, block_count, block_size, block_count, block_size)
    flat_acts = col_acts.reshape(-1, chan_width)
    flat_grads = col_grads.reshape(-1, chan_width)
    w_all = jnp.concatenate([w_query, w_key, w_value, w_gate], axis=1)
    projected = jnp.dot(flat_acts, w_all, preferred_element_type=jnp.float32)
    queries = (projected[:, :proj_width] * score_scale).astype(jnp.bfloat16)
    key_proj = projected[:, proj_width : 2 * proj_width].astype(jnp.bfloat16)
    values = projected[:, 2 * proj_width : 3 * proj_width].astype(jnp.bfloat16)
    gate_act = jax.nn.sigmoid(projected[:, 3 * proj_width :])
    d_gated = lax.dot_general(
        flat_grads, w_out, (((1,), (1,)), ((), ())), preferred_element_type=jnp.float32
    )
    block_shape = (block_count, block_size, col_width, head_count, head_dim)
    key_all = key_proj.reshape(block_shape)
    value_all = values.reshape(block_shape)
    slot_ids = jnp.arange(slot_count)
    scan_inputs = (
        queries.reshape(block_shape),
        gate_act.reshape(block_shape),
        d_gated.reshape(block_shape),
        jnp.arange(block_count, dtype=jnp.int32),
    )

    def per_block(running, inputs):
        dk_acc, dv_acc = running
        q_blk, g_blk, dg_blk, q_index = inputs
        chosen = key_blocks[q_index]
        live_slots = slot_ids < list_len[q_index]
        k_sel = jnp.take(key_all, chosen, axis=0)
        v_sel = jnp.take(value_all, chosen, axis=0)
        b_col = lax.dynamic_index_in_dim(bias_blocks, q_index, axis=3, keepdims=False)
        b_sel = jnp.take(b_col, chosen, axis=1)
        b_term = jnp.transpose(b_sel, (0, 3, 1, 2)).astype(jnp.float32)
        scores = (
            jnp.einsum("iwhd,ekwhd->whiek", q_blk, k_sel, preferred_element_type=jnp.float32)
            + b_term[None]
        )
        scores = jnp.where(live_slots[None, None, None, :, None], scores, -jnp.inf)
        row_peak = jnp.max(scores, axis=(3, 4), keepdims=True)
        exp_scores = jnp.exp(scores - row_peak)
        att_probs = exp_scores / jnp.sum(exp_scores, axis=(3, 4), keepdims=True)
        probs_low = att_probs.astype(jnp.bfloat16)
        attended = jnp.einsum(
            "whiek,ekwhd->iwhd", probs_low, v_sel, preferred_element_type=jnp.float32
        )
        gated = (g_blk * attended).astype(jnp.bfloat16)
        d_att = (dg_blk * g_blk).astype(jnp.bfloat16)
        d_gpre = (dg_blk * attended * g_blk * (1.0 - g_blk)).astype(jnp.bfloat16)
        d_probs = jnp.einsum("iwhd,ekwhd->whiek", d_att, v_sel, preferred_element_type=jnp.float32)
        delta_sum = jnp.sum(d_att.astype(jnp.float32) * attended, axis=-1)
        delta_sum = jnp.transpose(delta_sum, (1, 2, 0))[..., None, None]
        d_scores = att_probs * (d_probs - delta_sum)
        ds_low = d_scores.astype(jnp.bfloat16)
        d_query = (
            jnp.einsum("whiek,ekwhd->iwhd", ds_low, k_sel, preferred_element_type=jnp.float32)
            * score_scale
        ).astype(jnp.bfloat16)
        dk_part = jnp.einsum("whiek,iwhd->ekwhd", ds_low, q_blk, preferred_element_type=jnp.float32)
        dv_part = jnp.einsum(
            "whiek,iwhd->ekwhd", probs_low, d_att, preferred_element_type=jnp.float32
        )
        dk_acc = dk_acc.at[chosen].add(dk_part)
        dv_acc = dv_acc.at[chosen].add(dv_part)
        bias_part = jnp.transpose(jnp.sum(d_scores, axis=0), (2, 0, 3, 1))
        return ((dk_acc, dv_acc), (gated, d_query, d_gpre, bias_part))

    start = (jnp.zeros(block_shape, jnp.float32), jnp.zeros(block_shape, jnp.float32))
    (dk_acc, dv_acc), (gated, d_query, d_gpre, bias_parts) = lax.scan(per_block, start, scan_inputs)
    grads_all = jnp.concatenate(
        [
            d_query.reshape(-1, proj_width),
            dk_acc.astype(jnp.bfloat16).reshape(-1, proj_width),
            dv_acc.astype(jnp.bfloat16).reshape(-1, proj_width),
            d_gpre.reshape(-1, proj_width),
        ],
        axis=1,
    )
    d_flat = lax.dot_general(
        grads_all, w_all, (((1,), (1,)), ((), ())), preferred_element_type=jnp.float32
    ).astype(jnp.bfloat16)
    d_cols = d_flat.reshape(token_count, col_width, chan_width)
    d_pair = lax.all_to_all(d_cols, "row", split_axis=0, concat_axis=1, tiled=True)
    w_grad = lax.dot_general(
        flat_acts, grads_all, (((0,), (0,)), ((), ())), preferred_element_type=jnp.float32
    )
    o_grad = lax.dot_general(
        gated.reshape(-1, proj_width),
        flat_grads,
        (((0,), (0,)), ((), ())),
        preferred_element_type=jnp.float32,
    )
    block_match = (key_blocks[:, :, None] == jnp.arange(block_count)[None, None, :]).astype(
        jnp.float32
    )
    slot_form = jnp.transpose(bias_parts, (1, 2, 3, 0, 4)).reshape(
        slot_count, head_count, block_size, token_count
    )
    slot_cols = lax.psum_scatter(
        slot_form.astype(jnp.bfloat16), "col", scatter_dimension=3, tiled=True
    ).astype(jnp.float32)
    query_ids = lax.axis_index("col") * query_tile + jnp.arange(query_tile, dtype=jnp.int32)
    query_hit = ((query_ids // block_size)[:, None] == jnp.arange(block_count)[None, :]).astype(
        jnp.float32
    )
    slot_hit = jnp.einsum("iq,qeb->ebi", query_hit, block_match, precision=highest)
    expanded = jnp.einsum("ebi,ehki->hbki", slot_hit, slot_cols, precision=highest)
    expanded = expanded.reshape(head_count, token_count, query_tile)
    bias_grad = summed_on_arrival(expanded.astype(jnp.bfloat16), "row", 1)
    w_sum, o_sum = lax.psum((w_grad, o_grad), ("row", "col"))
    return (
        d_pair,
        bias_grad,
        w_sum[:, :proj_width],
        w_sum[:, proj_width : 2 * proj_width],
        w_sum[:, 2 * proj_width : 3 * proj_width],
        w_sum[:, 3 * proj_width :],
        o_sum,
    )


def solution(mesh):
    in_specs = (
        P("row", "col", None),
        P("row", "col", None),
        P(None, "row", "col"),
        P(),
        P(),
        P(),
        P(),
        P(),
        P(),
        P(),
    )
    out_specs = (P("row", "col", None), P(None, "row", "col"), P(), P(), P(), P(), P())
    return jax.shard_map(
        on_device, mesh=mesh, in_specs=in_specs, out_specs=out_specs, check_vma=False
    )
```

profile of v0, /device:TPU:1, one launch (start us, length us, event | category | flops | bytes accessed | tf_op | source)
XLA Modules:
  0.0 451.2 jit_solution(15507513807338690992)
XLA Ops:
  10.1 9.3 %all-to-all-start.1 = ((bf16[16,2,4096]{2,1,0:T(2,128)(2,1)}), bf16[16,2,4096]{2,1,0:T(2,128)(2,1)S(1)}, u32[]{:S(2)}, u32[]{:S(2)}) async-start(bf16[16,2,4096]{2,1,0:T(2,128)(2,1)} %reshape.201), calls=%async_computation.1 | async-start | bytes 524288 | tf_op jit(solution)/shard_map/all_to_all | solution.py:24
  21.0 7.3 %all-to-all-done.1 = bf16[16,2,4096]{2,1,0:T(2,128)(2,1)S(1)} async-done(((bf16[16,2,4096]{2,1,0:T(2,128)(2,1)}), bf16[16,2,4096]{2,1,0:T(2,128)(2,1)S(1)}, u32[]{:S(2)}, u32[]{:S(2)}) %all-to-all-start.1) | async-done | bytes 262176 | tf_op jit(solution)/shard_map/all_to_all | solution.py:24
  28.2 4.5 all-to-all-start
  33.5 15.1 %all-to-all-done = bf16[64,32,256]{2,0,1:T(8,128)(2,1)S(1)} async-done(((bf16[64,32,256]{2,0,1:T(8,128)(2,1)}), bf16[64,32,256]{2,0,1:T(8,128)(2,1)S(1)}, u32[]{:S(2)}, u32[]{:S(2)}) %all-to-all-start) | async-done | bytes 1048608 | tf_op jit(solution)/shard_map/all_to_all | solution.py:15
  50.2 4.4 all-to-all-start.2
  55.4 2.7 fusion.48
  58.9 1.8 reshape.132
  60.7 2.8 fusion.34
  64.4 2.6 copy.145
  67.0 1.9 reshape.130
  68.9 3.2 reshape.131
  72.1 4.7 %copy.147 = f32[4,128,4,4,32]{1,4,3,2,0:T(8,128)} copy(f32[4,128,4,4,32]{4,3,2,1,0:T(4,128)} %reshape.131) | data formatting | bytes 2097152
  78.1 3.6 all-to-all-done.2
  81.7 1.8 copy.143
  83.4 2.1 reshape_reshape.3
  85.5 3.5 copy.146
  91.8 164.2 %while.21 = (s32[]{:T(128)}, f32[4,128,4,4,32]{1,4,3,2,0:T(8,128)}, f32[4,128,4,4,32]{1,4,3,2,0:T(8,128)}, bf16[4,128,4,4,32]{1,4,3,2,0:T(8,128)(2,1)}, bf16[4,1...) while((s32[]{:T(128)}, f32[4,128,4,4,32]{1,4,3,2,0:T(8,128)}, ...), condition=%wide.region_7.9_spmd.clone, body=%wide.region_0.8_spmd.clone.sunk | while | flops 318042144 | bytes 61145636 | solution.py:135
  98.6 3.5 gather_fusion.1
  102.1 4.7 %gather_fusion = bf16[3,128,4,4,32]{4,3,2,1,0:T(4,128)(2,1)} fusion(bf16[4,128,4,4,32]{4,3,2,1,0:T(4,128)(2,1)} %get-tuple-element.471, s32[1024]{0:T(1024)S(1)} %pad_clamp_fusion.4), kind=kCustom, calls=%fused_computation.1.clone.clone.1 | custom fusion | bytes 786444 | tf_op jit(solution)/shard_map/while/body/eval_jaxpr/jit(_take)/gather | solution.py:97
  106.9 4.0 broadcast_select_fusion.3
  110.8 2.9 copy.209
  115.1 1.7 fusion.103
  118.4 2.2 multiply_reduce_fusion.2
  125.8 3.0 scatter_fusion
  129.8 2.2 fusion.107
  139.7 3.5 gather_fusion.1
  143.2 4.7 %gather_fusion = bf16[3,128,4,4,32]{4,3,2,1,0:T(4,128)(2,1)} fusion(bf16[4,128,4,4,32]{4,3,2,1,0:T(4,128)(2,1)} %get-tuple-element.471, s32[1024]{0:T(1024)S(1)} %pad_clamp_fusion.4), kind=kCustom, calls=%fused_computation.1.clone.clone.1 | custom fusion | bytes 786444 | tf_op jit(solution)/shard_map/while/body/eval_jaxpr/jit(_take)/gather | solution.py:97
  147.9 4.0 broadcast_select_fusion.3
  151.9 2.9 copy.209
  156.1 1.7 fusion.103
  159.4 2.2 multiply_reduce_fusion.2
  166.9 3.0 scatter_fusion
  170.9 2.2 fusion.107
  180.7 3.5 gather_fusion.1
  184.2 4.7 %gather_fusion = bf16[3,128,4,4,32]{4,3,2,1,0:T(4,128)(2,1)} fusion(bf16[4,128,4,4,32]{4,3,2,1,0:T(4,128)(2,1)} %get-tuple-element.471, s32[1024]{0:T(1024)S(1)} %pad_clamp_fusion.4), kind=kCustom, calls=%fused_computation.1.clone.clone.1 | custom fusion | bytes 786444 | tf_op jit(solution)/shard_map/while/body/eval_jaxpr/jit(_take)/gather | solution.py:97
  188.9 4.0 broadcast_select_fusion.3
  192.9 2.9 copy.209
  197.2 1.7 fusion.103
  200.5 2.2 multiply_reduce_fusion.2
  207.9 2.9 scatter_fusion
  211.9 2.2 fusion.107
  221.7 3.5 gather_fusion.1
  225.2 4.7 %gather_fusion = bf16[3,128,4,4,32]{4,3,2,1,0:T(4,128)(2,1)} fusion(bf16[4,128,4,4,32]{4,3,2,1,0:T(4,128)(2,1)} %get-tuple-element.471, s32[1024]{0:T(1024)S(1)} %pad_clamp_fusion.4), kind=kCustom, calls=%fused_computation.1.clone.clone.1 | custom fusion | bytes 786444 | tf_op jit(solution)/shard_map/while/body/eval_jaxpr/jit(_take)/gather | solution.py:97
  229.9 4.0 broadcast_select_fusion.3
  233.9 2.9 copy.209
  238.2 1.7 fusion.103
  241.5 2.2 multiply_reduce_fusion.2
  248.9 3.0 scatter_fusion
  252.9 2.2 fusion.107
  256.3 2.5 copy.161
  259.0 1.8 copy.150
  260.8 1.8 reshape.135
  262.6 1.8 copy.149
  264.4 1.8 reshape.134
  266.2 1.8 copy.160
  269.0 3.2 copy.148
  272.3 1.8 reshape.133
  274.0 1.8 copy.151
  275.8 1.7 reshape.136
  281.8 5.5 %all-to-all-start.3 = ((bf16[512,4,128]{2,1,0:T(4,128)(2,1)}), bf16[512,4,128]{2,1,0:T(4,128)(2,1)}, u32[]{:S(2)}, u32[]{:S(2)}) async-start(bf16[512,4,128]{2,1,0:T(4,128)(2,1)} %bitcast.239), calls=%async_computation.3 | async-start | bytes 1048576 | tf_op jit(solution)/shard_map/all_to_all | solution.py:149
  289.5 37.5 %reduce-scatter.2.cloned.1.call-done = bf16[3,4,128,32]{2,3,1,0:T(8,128)(2,1)} async-done(((bf16[3,4,128,512]{2,3,1,0:T(8,128)(2,1)}), bf16[3,4,128,32]{2,3,1,0:T(8,128)(2,1)}) %reduce-scatter.2.cloned.1.call-update) | async-done | bytes 98320 | tf_op jit(solution)/shard_map/reduce_scatter | solution.py:165
  329.5 4.1 all-to-all-start.4
  333.6 104.9 %all-reduce.3.cloned.1.call-done = (f32[128,512]{1,0:T(8,128)}, f32[128,128]{1,0:T(8,128)}) async-done(((f32[128,512]{1,0:T(8,128)}, f32[128,128]{1,0:T(8,128)}), (f32[128,512]{1,0:T(8,128)}, f32[128,128]{1,0:T(8,128)})) %all-reduce.3.cloned.1.call-update) | async-done | bytes 327696 | tf_op jit(solution)/shard_map/psum | solution.py:176
  440.2 2.0 copy.152
  (219 shorter events, 85.6 us)
Async XLA Ops:
  8.0 68.8 %copy-start = (bf16[128,128]{1,0:T(8,128)(2,1)S(1)}, bf16[128,128]{1,0:T(8,128)(2,1)}, u32[]{:S(2)}) copy-start(bf16[128,128]{1,0:T(8,128)(2,1)} %param.21) | copy-start | bytes 98308
  8.0 11.4 %copy-start.20 = (bf16[64,32,128]{2,1,0:T(8,128)(2,1)S(1)}, bf16[64,32,128]{2,1,0:T(8,128)(2,1)}, u32[]{:S(2)}) copy-start(bf16[64,32,128]{2,1,0:T(8,128)(2,1)} %param.14) | copy-start | bytes 1572868
  8.0 11.6 %copy-start.21 = (bf16[64,32,128]{2,1,0:T(8,128)(2,1)S(1)}, bf16[64,32,128]{2,1,0:T(8,128)(2,1)}, u32[]{:S(2)}) copy-start(bf16[64,32,128]{2,1,0:T(8,128)(2,1)} %param.15) | copy-start | bytes 1572868
  10.1 18.2 %all-to-all-start.1 = ((bf16[16,2,4096]{2,1,0:T(2,128)(2,1)}), bf16[16,2,4096]{2,1,0:T(2,128)(2,1)S(1)}, u32[]{:S(2)}, u32[]{:S(2)}) async-start(bf16[16,2,4096]{2,1,0:T(2,128)(2,1)} %reshape.201), calls=%async_computation.1 | async-start | bytes 524288 | tf_op jit(solution)/shard_map/all_to_all | solution.py:24
  19.8 12.9 %copy-start.23 = (bf16[128,128]{1,0:T(8,128)(2,1)S(1)}, bf16[128,128]{1,0:T(8,128)(2,1)}, u32[]{:S(2)}) copy-start(bf16[128,128]{1,0:T(8,128)(2,1)} %param.17) | copy-start | bytes 98308
  19.8 12.9 %copy-start.24 = (bf16[128,128]{1,0:T(8,128)(2,1)S(1)}, bf16[128,128]{1,0:T(8,128)(2,1)}, u32[]{:S(2)}) copy-start(bf16[128,128]{1,0:T(8,128)(2,1)} %param.18) | copy-start | bytes 98308
  19.8 13.0 %copy-start.25 = (bf16[128,128]{1,0:T(8,128)(2,1)S(1)}, bf16[128,128]{1,0:T(8,128)(2,1)}, u32[]{:S(2)}) copy-start(bf16[128,128]{1,0:T(8,128)(2,1)} %param.19) | copy-start | bytes 98308
  19.9 13.0 %copy-start.26 = (bf16[128,128]{1,0:T(8,128)(2,1)S(1)}, bf16[128,128]{1,0:T(8,128)(2,1)}, u32[]{:S(2)}) copy-start(bf16[128,128]{1,0:T(8,128)(2,1)} %param.20) | copy-start | bytes 98308
  28.2 20.3 %all-to-all-start = ((bf16[64,32,256]{2,0,1:T(8,128)(2,1)}), bf16[64,32,256]{2,0,1:T(8,128)(2,1)S(1)}, u32[]{:S(2)}, u32[]{:S(2)}) async-start(bf16[64,32,256]{2,0,1:T(8,128)(2,1)} %pad_maximum_fusion), calls=%async_computation | async-start | bytes 2097152 | tf_op jit(solution)/shard_map/all_to_all | solution.py:15
  32.9 22.5 %copy-start.16 = (bf16[128,512]{1,0:T(8,128)(2,1)}, bf16[128,512]{1,0:T(8,128)(2,1)S(1)}, u32[]{:S(2)}) copy-start(bf16[128,512]{1,0:T(8,128)(2,1)S(1)} %constant_dynamic-update-slice_fusion.1) | copy-start | bytes 393220
  50.2 31.5 %all-to-all-start.2 = ((bf16[8,4,64,512]{3,2,1,0:T(8,128)(2,1)}), bf16[8,4,64,512]{3,2,1,0:T(8,128)(2,1)}, u32[]{:S(2)}, u32[]{:S(2)}) async-start(bf16[8,4,64,512]{3,2,1,0:T(8,128)(2,1)} %broadcast_in_dim.75), calls=%async_computation.2 | async-start | bytes 4194304 | tf_op jit(solution)/shard_map/all_to_all | solution.py:24
  54.6 272.5 %reduce-scatter.2.cloned.1.call-start = ((), (), s32[]{:S(2)}) async-start(), calls=%async_computation.6 | async-start | bytes 1671168 | tf_op jit(solution)/shard_map/reduce_scatter | solution.py:165
  54.9 21.9 %copy-start.8 = (bf16[512,4,128]{2,0,1:T(8,128)(2,1)}, bf16[512,4,128]{2,0,1:T(8,128)(2,1)S(1)}, u32[]{:S(2)}) copy-start(bf16[512,4,128]{2,0,1:T(8,128)(2,1)S(1)} %get-tuple-element.285) | copy-start | bytes 1572868
  55.3 2.7 copy-start.9
  64.4 2.6 copy-start.15
  67.0 1.9 copy-start.11
  89.0 2.8 copy-start.27
  125.7 3.1 copy-start.2
  128.8 1.0 copy-start.7
  128.8 3.2 copy-start.6
  129.8 3.0 copy-start.3
  166.8 3.1 copy-start.2
  169.8 1.0 copy-start.7
  169.8 3.2 copy-start.6
  170.9 3.0 copy-start.3
  207.8 3.0 copy-start.2
  210.8 1.0 copy-start.7
  210.8 3.2 copy-start.6
  211.9 3.0 copy-start.3
  248.8 3.1 copy-start.2
  251.9 1.0 copy-start.7
  251.9 3.2 copy-start.6
  252.9 3.0 copy-start.3
  256.0 2.8 copy-start.5
  256.0 3.0 copy-start.4
  262.6 3.6 copy-start.19
  269.0 5.0 %copy-start.18 = (bf16[4,128,4,4,32]{1,4,3,2,0:T(8,128)(2,1)S(1)}, bf16[4,128,4,4,32]{1,4,3,2,0:T(8,128)(2,1)}, u32[]{:S(2)}) copy-start(bf16[4,128,4,4,32]{1,4,3,2,0:T(8,128)(2,1)} %get-tuple-element.103) | copy-start | bytes 1572868
  275.8 4.1 copy-start.12
  277.6 2.5 copy-start.13
  277.6 2.7 copy-start.17
  280.2 7.1 %copy-start.10 = (bf16[512,4,128]{2,1,0:T(4,128)(2,1)S(1)}, bf16[512,4,128]{2,1,0:T(4,128)(2,1)}, u32[]{:S(2)}) copy-start(bf16[512,4,128]{2,1,0:T(4,128)(2,1)} %copy-done.9) | copy-start | bytes 1572868
  281.8 47.7 %all-to-all-start.3 = ((bf16[512,4,128]{2,1,0:T(4,128)(2,1)}), bf16[512,4,128]{2,1,0:T(4,128)(2,1)}, u32[]{:S(2)}, u32[]{:S(2)}) async-start(bf16[512,4,128]{2,1,0:T(4,128)(2,1)} %bitcast.239), calls=%async_computation.3 | async-start | bytes 1048576 | tf_op jit(solution)/shard_map/all_to_all | solution.py:149
  287.3 151.2 %all-reduce.3.cloned.1.call-start = ((), (), s32[]{:S(2)}) async-start(), calls=%async_computation.7 | async-start | bytes 655360 | tf_op jit(solution)/shard_map/psum | solution.py:176
  287.3 1.2 copy-start.14
  327.1 116.7 %copy-start.1 = (bf16[128,128]{1,0:T(8,128)(2,1)S(1)}, bf16[128,128]{1,0:T(8,128)(2,1)}, u32[]{:S(2)}) copy-start(bf16[128,128]{1,0:T(8,128)(2,1)} %param.21) | copy-start | bytes 98308
  329.5 112.7 %all-to-all-start.4 = ((bf16[8,2,4096]{2,1,0:T(2,128)(2,1)}), bf16[8,2,4096]{2,1,0:T(2,128)(2,1)S(1)}, u32[]{:S(2)}, u32[]{:S(2)}) async-start(bf16[8,2,4096]{2,1,0:T(2,128)(2,1)} %reshape.203), calls=%async_computation.5 | async-start | bytes 262144 | tf_op jit(solution)/shard_map/all_to_all | solution.py:46
  438.5 4.6 %copy-start.22 = (f32[128,128]{1,0:T(8,128)S(1)}, f32[128,128]{1,0:T(8,128)}, u32[]{:S(2)}) copy-start(f32[128,128]{1,0:T(8,128)} %get-tuple-element.481) | copy-start | bytes 196612
Sparse Core Ops, SparseCore 0:
  256.1 70.8 reduce-scatter.1
Sparse Core Ops, SparseCore 1:
  293.3 145.2 all-reduce.2
where the time goes:
time: 454 us; the launch traced here: 451 us
  waiting for transfers between devices  168 us (37%)
  local copies, waits for them, and re-layouts  135 us (30%)
  other arithmetic  54.5 us (12%)
  matrix products  41 us (9%)
  starting transfers between devices  27.9 us (6%)
  between operations  16 us (4%)
  loops' own time  8.32 us (2%)
    psum x1, waiting for transfers between devices, on_device(): w_sum, o_sum = lax.psum((w_grad, o_grad), ('row', 'col'))  105 us
    reduce_scatter x1, waiting for transfers between devices, on_device(): lax.psum_scatter(slot_form.astype(jnp.bfloat16), 'col', scatter_dimension...  37.5 us
    gather x4, local copies, waits for them, and re-layouts, per_block(): v_sel = jnp.take(value_all, chosen, axis=0)  18.9 us
    unnamed x66, local copies, waits for them, and re-layouts  18 us
    select_n x4, other arithmetic, per_block(): v_sel = jnp.take(value_all, chosen, axis=0)  15.8 us
    all_to_all x1, waiting for transfers between devices, in_one_piece(): lax.all_to_all(both, axis, split_axis=split_dim, concat_axis=concat_dim,...  15.1 us
    gather x4, local copies, waits for them, and re-layouts, per_block(): k_sel = jnp.take(key_all, chosen, axis=0)  14 us
    all_to_all x2, starting transfers between devices, from_everyone(): lax.all_to_all(jnp.broadcast_to(x[None], (devices, *x.shape)), axis, 0, 0...  13.7 us
  transfers between devices with their start and end apart: 7, of which 5 were waited for; matrix products, arithmetic and copies ran while one was open for 13% of the time, Pallas kernels for 0%

commit v1 on v0

v1 whole, which is shorter than its diff:
```python
import jax
import jax.numpy as jnp
from jax import lax
from jax.experimental import pallas as pl
from jax.experimental.pallas import tpu as pltpu
from jax.sharding import PartitionSpec as P

BF = jnp.bfloat16
F32 = jnp.float32
HEADS = 4
HEAD_DIM = 32
PROJ = HEADS * HEAD_DIM
BLOCK = 128
QBLOCKS = 4
SLOTS = 3
TOKENS = QBLOCKS * BLOCK
WIDE = SLOTS * BLOCK
ALL = HEADS * WIDE
ROWS = 8
COLS = 16
TILE_ROWS = TOKENS // ROWS
TILE_COLS = TOKENS // COLS
COL_WIDTH = TILE_COLS // ROWS
WROWS = 5 * PROJ
WPART = WROWS // ROWS
DEAD = -1e30
SCALE = HEAD_DIM ** -0.5

ROW_OFFS = [(dz, dx) for dz in range(2) for dx in range(4)][1:]
COL_OFFS = [(dy, dz, dc) for dy in range(4) for dz in range(2) for dc in range(2)][1:]


def row_peer(r, off):
    z, x = r // 4, lax.rem(r, 4)
    return lax.rem(z + off[0], 2) * 4 + lax.rem(x + off[1], 4)


def col_peer(c, off):
    y, z, k = c // 4, lax.rem(c // 2, 2), lax.rem(c, 2)
    return lax.rem(y + off[0], 4) * 4 + lax.rem(z + off[1], 2) * 2 + lax.rem(k + off[2], 2)


def remote(src, dst, ssem, rsem, r, c):
    return pltpu.make_async_remote_copy(
        src_ref=src,
        dst_ref=dst,
        send_sem=ssem,
        recv_sem=rsem,
        device_id=(r, c),
        device_id_type=pl.DeviceIdType.MESH,
    )


def greet(r, c, col_offs):
    sem = pltpu.get_barrier_semaphore()
    for off in ROW_OFFS:
        pl.semaphore_signal(
            sem, inc=1, device_id=(row_peer(r, off), c), device_id_type=pl.DeviceIdType.MESH
        )
    for off in col_offs:
        pl.semaphore_signal(
            sem, inc=1, device_id=(r, col_peer(c, off)), device_id_type=pl.DeviceIdType.MESH
        )
    pl.semaphore_wait(sem, len(ROW_OFFS) + len(col_offs))


IN_COLS = [(0, 0, 1), (0, 1, 0), (1, 0, 0), (2, 0, 0), (3, 0, 0)]


def in_kernel(
    kb_ref, len_ref, act_ref, grad_ref, bias_ref, acol_ref, gcol_ref, full_ref,
    got, turned, mine, sa, ra, sg, rg, sb, rb, sz, rz, sc, rc, sy, ry, sf, rf, sl,
):
    r, c = lax.axis_index("row"), lax.axis_index("col")
    y = c // 4
    greet(r, c, IN_COLS)
    first = []
    for n, off in enumerate(ROW_OFFS):
        p = row_peer(r, off)
        cp = remote(bias_ref, got.at[r], sb.at[n], rb.at[n], p, c)
        cp.start()
        first.append(cp)
    rows = pl.ds(r * TILE_ROWS, TILE_ROWS)
    big = []
    for n, off in enumerate(ROW_OFFS):
        p = row_peer(r, off)
        part = pl.ds(p * COL_WIDTH, COL_WIDTH)
        ca = remote(act_ref.at[part], acol_ref.at[:, rows, :], sa.at[n], ra.at[n], p, c)
        cg = remote(grad_ref.at[part], gcol_ref.at[:, rows, :], sg.at[n], rg.at[n], p, c)
        ca.start()
        cg.start()
        big += [ca, cg]
    own = pl.ds(r * COL_WIDTH, COL_WIDTH)
    la = pltpu.make_async_copy(act_ref.at[own], acol_ref.at[:, rows, :], sl.at[0])
    lg = pltpu.make_async_copy(grad_ref.at[own], gcol_ref.at[:, rows, :], sl.at[1])
    la.start()
    lg.start()
    got[r] = bias_ref[...]
    for cp in first:
        cp.wait()
    for k in range(QBLOCKS):
        pair = jnp.concatenate([got[2 * k], got[2 * k + 1]], axis=0).astype(F32)
        turned[k] = pair.T.astype(BF)
    for s in range(SLOTS):
        tile = turned[kb_ref[y, s]]
        tile = jnp.where(s < len_ref[y], tile.astype(F32), DEAD).astype(BF)
        for h in range(HEADS):
            mine[:, h * WIDE + s * BLOCK : h * WIDE + (s + 1) * BLOCK] = tile[
                h * HEAD_DIM : (h + 1) * HEAD_DIM, :
            ]

    def piece(cc):
        return full_ref.at[pl.ds(cc * TILE_COLS, TILE_COLS), :]

    sends = []
    zc = col_peer(c, (0, 1, 0))
    sib = col_peer(c, (0, 0, 1))
    cz = remote(mine, piece(c), sz.at[0], rz.at[0], r, zc)
    cz.start()
    to_y = []
    for n in range(3):
        cp = remote(mine, piece(c), sy.at[n], ry.at[n], r, col_peer(c, (n + 1, 0, 0)))
        cp.start()
        to_y.append(cp)
    cs = remote(mine, piece(c), sc.at[0], rc.at[0], r, sib)
    cs.start()
    lm = pltpu.make_async_copy(mine, piece(c), sl.at[2])
    lm.start()

    def forward(n, cc):
        cp = remote(piece(cc), piece(cc), sf.at[n], rf.at[n], r, sib)
        cp.start()
        sends.append(cp)

    cz.wait_recv()
    for n in range(3):
        cp = remote(piece(zc), piece(zc), sy.at[3 + n], ry.at[3 + n], r, col_peer(c, (n + 1, 0, 0)))
        cp.start()
        to_y.append(cp)
    forward(0, zc)
    for n in range(3):
        to_y[n].wait_recv()
        forward(1 + n, col_peer(c, (3 - n, 0, 0)))
    for n in range(3):
        to_y[3 + n].wait_recv()
        forward(4 + n, col_peer(c, (3 - n, 1, 0)))
    cz.wait_send()
    for cp in to_y:
        cp.wait_send()
    cs.wait()
    for cp in sends:
        cp.wait()
    for cp in big:
        cp.wait()
    la.wait()
    lg.wait()
    lm.wait()


def gather_in(key_blocks, list_len, act, grad, bias):
    any_ = pl.BlockSpec(memory_space=pl.ANY)
    smem = pl.BlockSpec(memory_space=pltpu.SMEM)
    vmem = pl.BlockSpec(memory_space=pltpu.VMEM)
    dma = pltpu.SemaphoreType.DMA
    return pl.pallas_call(
        in_kernel,
        out_shape=(
            jax.ShapeDtypeStruct((COL_WIDTH, TOKENS, PROJ), BF),
            jax.ShapeDtypeStruct((COL_WIDTH, TOKENS, PROJ), BF),
            jax.ShapeDtypeStruct((TOKENS, ALL), BF),
        ),
        in_specs=[smem, smem, any_, any_, vmem],
        out_specs=(any_, any_, any_),
        scratch_shapes=[
            pltpu.VMEM((ROWS, TILE_ROWS, PROJ), BF),
            pltpu.VMEM((QBLOCKS, PROJ, BLOCK), BF),
            pltpu.VMEM((TILE_COLS, ALL), BF),
            dma((7,)), dma((7,)), dma((7,)), dma((7,)), dma((7,)), dma((7,)),
            dma((1,)), dma((1,)), dma((1,)), dma((1,)), dma((6,)), dma((6,)), dma((7,)), dma((7,)),
            dma((3,)),
        ],
        compiler_params=pltpu.CompilerParams(collective_id=0, has_side_effects=True),
        name="gather_in",
    )(key_blocks, list_len, act, grad, bias)


NT = (((1,), (1,)), ((), ()))
NN = (((1,), (0,)), ((), ()))


def mm(a, b, dims=NN):
    return lax.dot_general(a, b, dims, preferred_element_type=F32)


def main_kernel(
    kb_ref, act_ref, grad_ref, bias_ref, w_ref, wo_ref, dpair_ref, dbias_ref, dw_ref,
    q_s, k_s, v_s, g_s, dg_s, dq_s, dgp_s, gated_s, dkt_s, dvt_s, dacc_s, dw_s, dwo_s,
):
    head_of = lax.broadcasted_iota(jnp.int32, (BLOCK, PROJ), 1) // HEAD_DIM
    masks = [(head_of == h) for h in range(HEADS)]

    @pl.loop(0, COL_WIDTH)
    def _(w):
        proj = mm(act_ref[w], w_ref[...])
        q_s[w] = (proj[:, :PROJ] * SCALE).astype(BF)
        k_s[w] = proj[:, PROJ : 2 * PROJ].astype(BF)
        v_s[w] = proj[:, 2 * PROJ : 3 * PROJ].astype(BF)
        g_s[w] = jax.nn.sigmoid(proj[:, 3 * PROJ :])
        dg_s[w] = mm(grad_ref[w], wo_ref[...], NT)
        dkt_s[w] = jnp.zeros((PROJ, TOKENS), F32)
        dvt_s[w] = jnp.zeros((PROJ, TOKENS), F32)

    dw_s[...] = jnp.zeros_like(dw_s)
    dwo_s[...] = jnp.zeros_like(dwo_s)

    @pl.loop(0, QBLOCKS * COL_WIDTH)
    def _(t):
        b, w = t // COL_WIDTH, lax.rem(t, COL_WIDTH)
        rows = pl.ds(pl.multiple_of(b * BLOCK, BLOCK), BLOCK)
        kbs = [pl.multiple_of(kb_ref[b, s] * BLOCK, BLOCK) for s in range(SLOTS)]
        q = q_s[w, rows, :]
        ks = [k_s[w, pl.ds(kb, BLOCK), :] for kb in kbs]
        vs = [v_s[w, pl.ds(kb, BLOCK), :] for kb in kbs]
        zero = jnp.zeros((BLOCK, PROJ), BF)
        one = jnp.ones((BLOCK, PROJ), BF)
        k4 = jnp.concatenate([jnp.where(m, x, zero) for m in masks for x in ks], axis=0)
        v4 = jnp.concatenate([jnp.where(m, x, zero) for m in masks for x in vs], axis=0)
        m4 = jnp.concatenate([jnp.where(m, one, zero) for m in masks for _ in vs], axis=0)
        vm4 = jnp.concatenate([v4, m4], axis=1)
        scores = mm(q, k4, NT) + bias_ref[rows, :].astype(F32)
        es = []
        for h in range(HEADS):
            sh = scores[:, h * WIDE : (h + 1) * WIDE]
            es.append(jnp.exp(sh - jnp.max(sh, axis=1, keepdims=True)))
        e = jnp.concatenate(es, axis=1)
        e_low = e.astype(BF)
        both = mm(e_low, vm4)
        inv = 1.0 / both[:, PROJ:]
        att = both[:, :PROJ] * inv
        g = g_s[w, rows, :]
        dg = dg_s[w, rows, :]
        gated_s[w, rows, :] = (g * att).astype(BF)
        datt = dg * g
        dgp_s[w, rows, :] = (datt * att * (1.0 - g)).astype(BF)
        datt_n = (datt * inv).astype(BF)
        prod = datt_n.astype(F32) * att
        dp = mm(datt_n, v4, NT)
        dss = []
        for h in range(HEADS):
            delta = jnp.sum(jnp.where(masks[h], prod, 0.0), axis=1, keepdims=True)
            dss.append(es[h] * (dp[:, h * WIDE : (h + 1) * WIDE] - delta))
        ds = jnp.concatenate(dss, axis=1)
        ds_low = ds.astype(BF)

        @pl.when(w == 0)
        def _():
            dacc_s[...] = ds

        @pl.when((w > 0) & (w < COL_WIDTH - 1))
        def _():
            dacc_s[...] += ds

        @pl.when(w == COL_WIDTH - 1)
        def _():
            dbias_ref[rows, :] = (dacc_s[...] + ds).astype(BF)

        dq_s[w, rows, :] = (mm(ds_low, k4) * SCALE).astype(BF)
        qt = q.astype(F32).T.astype(BF)
        dt = datt_n.astype(F32).T.astype(BF)
        dk, dv = [], []
        for h in range(HEADS):
            hs = slice(h * HEAD_DIM, (h + 1) * HEAD_DIM)
            ws = slice(h * WIDE, (h + 1) * WIDE)
            dk.append(mm(qt[hs], ds_low[:, ws]))
            dv.append(mm(dt[hs], e_low[:, ws]))
        dk = jnp.concatenate(dk, axis=0)
        dv = jnp.concatenate(dv, axis=0)
        for s in range(SLOTS):
            lanes = pl.ds(kbs[s], BLOCK)
            dkt_s[w, :, lanes] += dk[:, s * BLOCK : (s + 1) * BLOCK]
            dvt_s[w, :, lanes] += dv[:, s * BLOCK : (s + 1) * BLOCK]

    @pl.loop(0, COL_WIDTH)
    def _(w):
        dk = dkt_s[w].T.astype(BF)
        dv = dvt_s[w].T.astype(BF)
        grads = jnp.concatenate([dq_s[w], dk, dv, dgp_s[w]], axis=1)
        dpair_ref[w] = mm(grads, w_ref[...], NT).astype(BF)
        xt = act_ref[w].astype(F32).T.astype(BF)
        dw_s[...] += mm(xt, grads)
        gt = gated_s[w].astype(F32).T.astype(BF)
        dwo_s[...] += mm(gt, grad_ref[w])

    for n in range(4):
        dw_ref[n * PROJ : (n + 1) * PROJ, :] = dw_s[:, n * PROJ : (n + 1) * PROJ].astype(BF)
    dw_ref[4 * PROJ :, :] = dwo_s[...].astype(BF)


def compute(key_blocks, acol, gcol, full, w_all, w_out):
    smem = pl.BlockSpec(memory_space=pltpu.SMEM)
    vmem = pl.BlockSpec(memory_space=pltpu.VMEM)
    cols = (COL_WIDTH, TOKENS, PROJ)
    return pl.pallas_call(
        main_kernel,
        out_shape=(
            jax.ShapeDtypeStruct(cols, BF),
            jax.ShapeDtypeStruct((TOKENS, ALL), BF),
            jax.ShapeDtypeStruct((WROWS, PROJ), BF),
        ),
        in_specs=[smem] + [vmem] * 5,
        out_specs=(vmem, vmem, vmem),
        scratch_shapes=[
            pltpu.VMEM(cols, BF), pltpu.VMEM(cols, BF), pltpu.VMEM(cols, BF),
            pltpu.VMEM(cols, F32), pltpu.VMEM(cols, F32),
            pltpu.VMEM(cols, BF), pltpu.VMEM(cols, BF), pltpu.VMEM(cols, BF),
            pltpu.VMEM((COL_WIDTH, PROJ, TOKENS), F32), pltpu.VMEM((COL_WIDTH, PROJ, TOKENS), F32),
            pltpu.VMEM((BLOCK, ALL), F32),
            pltpu.VMEM((PROJ, 4 * PROJ), F32), pltpu.VMEM((PROJ, PROJ), F32),
        ],
        name="attend_back",
    )(key_blocks, acol, gcol, full, w_all, w_out)


def out_kernel(
    kb_ref, len_ref, dpair_ref, part_ref, dw_ref, dp_ref, db_ref, wsum_ref,
    r1, s1, r2, s2, r3, dense, r4, r5, s6, w6,
    sd, rd, a1, b1, a2, b2, a3, b3, a4, b4, a5, b5, a6, b6, a7, b7, sl,
):
    r, c = lax.axis_index("row"), lax.axis_index("col")
    y, zh, core = c // 4, lax.rem(c // 2, 2), lax.rem(c, 2)
    greet(r, c, COL_OFFS)
    sib = col_peer(c, (0, 0, 1))
    c1 = []
    for n in range(8):
        yy = lax.rem(y + 1 + n // 2, 4)
        cc = yy * 4 + (n % 2) * 2
        src = part_ref.at[pl.ds((cc + 1 - core) * TILE_COLS, TILE_COLS), :]
        cp = remote(src, r1.at[n], a1.at[n], b1.at[n], r, sib)
        cp.start()
        c1.append(cp)
    c5 = []
    for n, off in enumerate(ROW_OFFS):
        p = row_peer(r, off)
        cp = remote(dw_ref.at[pl.ds(p * WPART, WPART), :], r5.at[n], a5.at[n], b5.at[n], p, c)
        cp.start()
        c5.append(cp)
    cd = []
    mycols = pl.ds(r * COL_WIDTH, COL_WIDTH)
    for n, off in enumerate(ROW_OFFS):
        p = row_peer(r, off)
        src = dpair_ref.at[:, pl.ds(p * TILE_ROWS, TILE_ROWS), :]
        cp = remote(src, dp_ref.at[mycols], sd.at[n], rd.at[n], p, c)
        cp.start()
        cd.append(cp)
    ld = pltpu.make_async_copy(
        dpair_ref.at[:, pl.ds(r * TILE_ROWS, TILE_ROWS), :], dp_ref.at[mycols], sl.at[0]
    )
    ld.start()
    c2 = []
    for n in range(8):
        c1[n].wait_recv()
        yy = lax.rem(y + 1 + n // 2, 4)
        cc = yy * 4 + (n % 2) * 2 + core
        own = part_ref[pl.ds(cc * TILE_COLS, TILE_COLS), :]
        s1[n] = (own.astype(F32) + r1[n].astype(F32)).astype(BF)
        if n < 6 and n % 2 == 1:
            m = n // 2
            cp = remote(
                s1.at[pl.ds(2 * m, 2)], r2.at[m], a2.at[m], b2.at[m], r, col_peer(c, (m + 1, 0, 0))
            )
            cp.start()
            c2.append(cp)
    for cp in c5:
        cp.wait_recv()
    tot = dw_ref[pl.ds(r * WPART, WPART), :].astype(F32)
    for n in range(7):
        tot = tot + r5[n].astype(F32)
    s6[...] = tot.astype(BF)
    w6[c] = s6[...]
    c6 = []
    for n, off in enumerate(COL_OFFS):
        cp = remote(s6, w6.at[c], a6.at[n], b6.at[n], r, col_peer(c, off))
        cp.start()
        c6.append(cp)
    for cp in c2:
        cp.wait_recv()
    other = 1 - zh
    acc = s1[6 + other].astype(F32)
    for m in range(3):
        acc = acc + r2[m, other].astype(F32)
    s2[...] = acc.astype(BF)
    c3 = remote(s2, r3, a3.at[0], b3.at[0], r, col_peer(c, (0, 1, 0)))
    c3.start()
    acc = s1[6 + zh].astype(F32)
    for m in range(3):
        acc = acc + r2[m, zh].astype(F32)
    for cp in c6:
        cp.wait_recv()
    tot = w6[0].astype(F32)
    for n in range(1, COLS):
        tot = tot + w6[n].astype(F32)
    myrows = pl.ds(r * WPART, WPART)
    wsum_ref[myrows, :] = tot
    c7 = []
    for n, off in enumerate(ROW_OFFS):
        cp = remote(
            wsum_ref.at[myrows, :], wsum_ref.at[myrows, :], a7.at[n], b7.at[n], row_peer(r, off), c
        )
        cp.start()
        c7.append(cp)
    c3.wait_recv()
    acc = acc + r3[...].astype(F32)
    turned = []
    for s in range(SLOTS):
        tile = jnp.concatenate(
            [acc[:, h * WIDE + s * BLOCK : h * WIDE + (s + 1) * BLOCK] for h in range(HEADS)], axis=0
        )
        turned.append(tile.T)
    for k in range(QBLOCKS):
        val = jnp.zeros((BLOCK, PROJ), F32)
        for s in range(SLOTS):
            hit = (kb_ref[y, s] == k) & (s < len_ref[y])
            val = val + jnp.where(hit, turned[s], 0.0)
        dense[k * BLOCK : (k + 1) * BLOCK, :] = val.astype(BF)
    c4 = []
    for n, off in enumerate(ROW_OFFS):
        p = row_peer(r, off)
        cp = remote(dense.at[pl.ds(p * TILE_ROWS, TILE_ROWS), :], r4.at[n], a4.at[n], b4.at[n], p, c)
        cp.start()
        c4.append(cp)
    val = dense[pl.ds(r * TILE_ROWS, TILE_ROWS), :].astype(F32)
    for n in range(7):
        c4[n].wait_recv()
        val = val + r4[n].astype(F32)
    db_ref[...] = val
    for cp in c7 + cd:
        cp.wait_recv()
    for cp in c1 + c2 + [c3] + c4 + c5 + c6 + c7 + cd:
        cp.wait_send()
    ld.wait()


def send_out(key_blocks, list_len, dpair, part, dw):
    any_ = pl.BlockSpec(memory_space=pl.ANY)
    smem = pl.BlockSpec(memory_space=pltpu.SMEM)
    vmem = pl.BlockSpec(memory_space=pltpu.VMEM)
    dma = pltpu.SemaphoreType.DMA
    piece = (TILE_COLS, ALL)
    return pl.pallas_call(
        out_kernel,
        out_shape=(
            jax.ShapeDtypeStruct((TILE_COLS, TILE_ROWS, PROJ), BF),
            jax.ShapeDtypeStruct((TILE_ROWS, PROJ), F32),
            jax.ShapeDtypeStruct((WROWS, PROJ), F32),
        ),
        in_specs=[smem, smem, any_, vmem, vmem],
        out_specs=(any_, vmem, vmem),
        scratch_shapes=[
            pltpu.VMEM((8, *piece), BF), pltpu.VMEM((8, *piece), BF),
            pltpu.VMEM((3, 2, *piece), BF), pltpu.VMEM(piece, BF), pltpu.VMEM(piece, BF),
            pltpu.VMEM((TOKENS, PROJ), BF), pltpu.VMEM((7, TILE_ROWS, PROJ), BF),
            pltpu.VMEM((7, WPART, PROJ), BF), pltpu.VMEM((WPART, PROJ), BF),
            pltpu.VMEM((COLS, WPART, PROJ), BF),
            dma((7,)), dma((7,)), dma((8,)), dma((8,)), dma((3,)), dma((3,)), dma((1,)), dma((1,)),
            dma((7,)), dma((7,)), dma((7,)), dma((7,)), dma((15,)), dma((15,)), dma((7,)), dma((7,)),
            dma((1,)),
        ],
        compiler_params=pltpu.CompilerParams(collective_id=1, has_side_effects=True),
        name="send_out",
    )(key_blocks, list_len, dpair, part, dw)


def on_device(
    pair_act, out_grad, tri_bias, w_query, w_key, w_value, w_gate, w_out, key_blocks, list_len
):
    act = jnp.transpose(pair_act, (1, 0, 2))
    grad = jnp.transpose(out_grad, (1, 0, 2))
    bias = jnp.transpose(tri_bias, (1, 0, 2)).reshape(TILE_ROWS, PROJ)
    w_all = jnp.concatenate([w_query, w_key, w_value, w_gate], axis=1)
    acol, gcol, full = gather_in(key_blocks, list_len, act, grad, bias)
    dpair, part, dw = compute(key_blocks, acol, gcol, full, w_all, w_out)
    dp, db, ws = send_out(key_blocks, list_len, dpair, part, dw)
    d_pair = jnp.transpose(dp, (1, 0, 2))
    d_bias = jnp.transpose(db.reshape(TILE_ROWS, HEADS, TILE_COLS), (1, 0, 2))
    return (d_pair, d_bias) + tuple(ws[n * PROJ : (n + 1) * PROJ] for n in range(5))


def solution(mesh):
    in_specs = (
        P("row", "col", None), P("row", "col", None), P(None, "row", "col"),
        P(), P(), P(), P(), P(), P(), P(),
    )
    out_specs = (P("row", "col", None), P(None, "row", "col"), P(), P(), P(), P(), P())
    return jax.shard_map(
        on_device, mesh=mesh, in_specs=in_specs, out_specs=out_specs, check_vma=False
    )
```

time: 454 us -> 105 us (0.23)
  waiting for transfers between devices: 168 us -> 0 us
  local copies, waits for them, and re-layouts: 135 us -> 9.37 us
  Pallas kernels: 0 us -> 92.5 us
  other arithmetic: 54.5 us -> 1.48 us
  matrix products: 41 us -> 0 us
  starting transfers between devices: 27.9 us -> 0 us
  between operations: 16 us -> 0.65 us
  loops' own time: 8.32 us -> 0 us
    psum x1 -> x0, waiting for transfers between devices: 105 us -> none  [on_device(): w_sum, o_sum = lax.psum((w_grad, o_grad), ('row', 'col'))]
    pallas_call x0 -> x3, Pallas kernels: none -> 92.5 us  [the longest x1 37.5 us: send_out(): pl.pallas_call(out_kernel, out_shape=(jax.ShapeDtypeStruct((TILE_COLS, TI...]
    dot_general x31 -> x0, matrix products: 41 us -> none  [the longest x4 8.71 us: per_block(): jnp.einsum('whiek,ekwhd->iwhd', probs_low, v_sel, preferred_element_type=...]
    reduce_scatter x1 -> x0, waiting for transfers between devices: 37.5 us -> none  [on_device(): lax.psum_scatter(slot_form.astype(jnp.bfloat16), 'col', scatter_dimension...]
    gather x12 -> x0, local copies, waits for them, and re-layouts: 35.3 us -> none  [the longest x4 18.9 us: per_block(): v_sel = jnp.take(value_all, chosen, axis=0)]
    all_to_all x5 -> x0, starting transfers between devices: 27.8 us -> none  [the longest x2 13.7 us: from_everyone(): lax.all_to_all(jnp.broadcast_to(x[None], (devices, *x.shape)), axis, 0, 0...]
    all_to_all x5 -> x0, waiting for transfers between devices: 25.9 us -> none  [the longest x1 15.1 us: in_one_piece(): lax.all_to_all(both, axis, split_axis=split_dim, concat_axis=concat_dim,...]
    select_n x8 -> x0, local copies, waits for them, and re-layouts: 17.1 us -> none  [the longest x4 11.6 us: per_block(): k_sel = jnp.take(key_all, chosen, axis=0)]
  transfers between devices with their start and end apart: 7 -> 0, of which waited for: 5 -> 0; matrix products, arithmetic and copies ran while one was open for 13% -> 0% of each run, Pallas kernels for 0% -> 0%
where the time goes in v1:
time: 105 us; the launch traced here: 104 us
  Pallas kernels  92.5 us (88%)
  local copies, waits for them, and re-layouts  9.37 us (9%)
  other arithmetic  1.48 us (1%)
    pallas_call x1, Pallas kernels, send_out(): pl.pallas_call(out_kernel, out_shape=(jax.ShapeDtypeStruct((TILE_COLS, TI...  37.5 us
    pallas_call x1, Pallas kernels, compute(): pl.pallas_call(main_kernel, out_shape=(jax.ShapeDtypeStruct(cols, BF), ja...  27.8 us
    pallas_call x1, Pallas kernels, gather_in(): pl.pallas_call(in_kernel, out_shape=(jax.ShapeDtypeStruct((COL_WIDTH, TOK...  27.2 us
    transpose x1, local copies, waits for them, and re-layouts, on_device(): grad = jnp.transpose(out_grad, (1, 0, 2))  2.57 us
    unnamed x1, local copies, waits for them, and re-layouts  2.18 us

profile of v1, /device:TPU:1, one launch (start us, length us, event | category | flops | bytes accessed | tf_op | source)
XLA Modules:
  0.0 104.0 jit_solution(6061631675220014857)
XLA Ops:
  0.6 1.4 %copy.24.bias_ref = bf16[64,128]{1,0:T(8,128)(2,1)} copy(bf16[64,128]{0,1:T(8,128)(2,1)} %bitcast.13) | data formatting | bytes 32768 | tf_op jit(solution)/shard_map/reshape | solution.py:478
  2.1 1.5 %pad_maximum_fusion.w_ref = bf16[128,512]{1,0:T(8,128)(2,1)} fusion(bf16[128,128]{1,0:T(8,128)(2,1)} %param.16, bf16[128,128]{1,0:T(8,128)(2,1)} %param.15, bf16[128,128]{1,0:T(8,128)(2,1)} %param.14, bf16[128,128]{1,0:T(8,128)(2,1)} %param.13), kind=kLoop, calls=%fused_computation.2 | loop fusion | flops 524288 | bytes 262144 | tf_op jit(solution)/shard_map/concatenate | solution.py:479
  3.6 2.6 %copy_bitcast_fusion = (bf16[32,64,128]{2,1,0:T(8,128)(2,1)}, bf16[32,64,128]{2,1,0:T(8,128)(2,1)}) fusion(bf16[64,32,128]{2,1,0:T(8,128)(2,1)} %param.11, bf16[64,32,128]{2,1,0:T(8,128)(2,1)} %param.10), kind=kLoop, calls=%fused_computation | loop fusion | bytes 2097152 | tf_op jit(solution)/shard_map/transpose | solution.py:477
  6.1 27.2 %gather_in.1 = (bf16[4,512,128]{2,1,0:T(8,128)(2,1)}, bf16[4,512,128]{2,1,0:T(8,128)(2,1)}, bf16[512,1536]{1,0:T(8,128)(2,1)}) custom-call(s32[4,3]{1,0:T(4,128)} %kb_ref.5, s32[4]{0:T(128)} %len_ref.3, bf16[32,64,128]{2,1,0:T(8,128)(2,1)} %get-tuple-element.45.act_ref, bf16[32,64,128]{2,1,0:T(8,128)(2,1)} %get-tuple-element.44.grad_ref, ...), custom_call_target="tpu_custom_call" | custom-call | tf_op jit(solution)/shard_map/gather_in/pallas_call | solution.py:165
  33.3 27.8 %attend_back.1 = (bf16[4,512,128]{2,1,0:T(8,128)(2,1)}, bf16[512,1536]{1,0:T(8,128)(2,1)}, bf16[640,128]{1,0:T(8,128)(2,1)}) custom-call(s32[4,3]{1,0:T(4,128)} %kb_ref.5, bf16[4,512,128]{2,1,0:T(8,128)(2,1)} %get-tuple-element.16.act_ref, bf16[4,512,128]{2,1,0:T(8,128)(2,1)} %get-tuple-element.17.grad_ref, bf16[512,1536]{1,0:T(8,128)(2,1)} %get-tuple-element.18.bias_ref, ...), custom_call_target="tpu_custom_call" | custom-call | tf_op jit(solution)/shard_map/attend_back/pallas_call | solution.py:303
  61.2 37.5 %send_out.1 = (bf16[32,64,128]{2,1,0:T(8,128)(2,1)}, f32[64,128]{1,0:T(8,128)}, f32[640,128]{1,0:T(8,128)}) custom-call(s32[4,3]{1,0:T(4,128)} %kb_ref.5, s32[4]{0:T(128)} %len_ref.3, bf16[4,512,128]{2,1,0:T(8,128)(2,1)} %get-tuple-element.19.dpair_ref, bf16[512,1536]{1,0:T(8,128)(2,1)} %get-tuple-element.20.part_ref, bf16[640,128]{1,0:T(8,128)(2,1)} %get-tuple-element.21.dw_ref), custom_call_target="tpu_custom_call" | custom-call | tf_op jit(solution)/shard_map/send_out/pallas_call | solution.py:449
  98.7 2.2 %copy.26 = bf16[64,32,128]{2,1,0:T(8,128)(2,1)} copy(bf16[64,32,128]{2,0,1:T(8,128)(2,1)} %bitcast.11) | data formatting | bytes 1048576
  100.9 1.5 %copy.25 = f32[64,128]{0,1:T(8,128)} copy(f32[64,128]{1,0:T(8,128)} %get-tuple-element.23) | data formatting | bytes 65536 | tf_op jit(solution)/shard_map/send_out/pallas_call | solution.py:449
  102.3 1.7 %fusion = (f32[128,128]{1,0:T(8,128)}, f32[128,128]{1,0:T(8,128)}, f32[128,128]{1,0:T(8,128)}, f32[128,128]{1,0:T(8,128)}, f32[128,128]{1,0:T(8,128)}) fusion(f32[640,128]{1,0:T(8,128)} %get-tuple-element.24), kind=kLoop, calls=%fused_computation.3 | loop fusion | bytes 655360 | tf_op jit(solution)/shard_map/slice | solution.py:485

commit v2 on v1

--- a/solution.py
+++ b/solution.py
@@ -15,7 +15,6 @@
 SLOTS = 3
 TOKENS = QBLOCKS * BLOCK
 WIDE = SLOTS * BLOCK
-ALL = HEADS * WIDE
 ROWS = 8
 COLS = 16
 TILE_ROWS = TOKENS // ROWS
@@ -24,6 +23,7 @@
 WROWS = 5 * PROJ
 WPART = WROWS // ROWS
 DEAD = -1e30
+UNROLL = 1
 SCALE = HEAD_DIM ** -0.5
 
 ROW_OFFS = [(dz, dx) for dz in range(2) for dx in range(4)][1:]
@@ -104,13 +104,11 @@
     for s in range(SLOTS):
         tile = turned[kb_ref[y, s]]
         tile = jnp.where(s < len_ref[y], tile.astype(F32), DEAD).astype(BF)
-        for h in range(HEADS):
-            mine[:, h * WIDE + s * BLOCK : h * WIDE + (s + 1) * BLOCK] = tile[
-                h * HEAD_DIM : (h + 1) * HEAD_DIM, :
-            ]
+        mine[:, :, s * BLOCK : (s + 1) * BLOCK] = tile.reshape(HEADS, TILE_COLS, BLOCK)
 
     def piece(cc):
-        return full_ref.at[pl.ds(cc * TILE_COLS, TILE_COLS), :]
+        at = pl.multiple_of(lax.rem(cc, 4) * TILE_COLS, TILE_COLS)
+        return full_ref.at[cc // 4, :, pl.ds(at, TILE_COLS), :]
 
     sends = []
     zc = col_peer(c, (0, 1, 0))
@@ -167,14 +165,14 @@
         out_shape=(
             jax.ShapeDtypeStruct((COL_WIDTH, TOKENS, PROJ), BF),
             jax.ShapeDtypeStruct((COL_WIDTH, TOKENS, PROJ), BF),
-            jax.ShapeDtypeStruct((TOKENS, ALL), BF),
+            jax.ShapeDtypeStruct((QBLOCKS, HEADS, BLOCK, WIDE), BF),
         ),
         in_specs=[smem, smem, any_, any_, vmem],
         out_specs=(any_, any_, any_),
         scratch_shapes=[
             pltpu.VMEM((ROWS, TILE_ROWS, PROJ), BF),
             pltpu.VMEM((QBLOCKS, PROJ, BLOCK), BF),
-            pltpu.VMEM((TILE_COLS, ALL), BF),
+            pltpu.VMEM((HEADS, TILE_COLS, WIDE), BF),
             dma((7,)), dma((7,)), dma((7,)), dma((7,)), dma((7,)), dma((7,)),
             dma((1,)), dma((1,)), dma((1,)), dma((1,)), dma((6,)), dma((6,)), dma((7,)), dma((7,)),
             dma((3,)),
@@ -193,132 +191,193 @@
 
 
 def main_kernel(
-    kb_ref, act_ref, grad_ref, bias_ref, w_ref, wo_ref, dpair_ref, dbias_ref, dw_ref,
-    q_s, k_s, v_s, g_s, dg_s, dq_s, dgp_s, gated_s, dkt_s, dvt_s, dacc_s, dw_s, dwo_s,
+    kb_ref, len_ref, act_ref, grad_ref, bias_ref, wq_ref, wk_ref, wv_ref, wg_ref, wo_ref,
+    dpair_ref, dbias_ref, dw_ref,
+    wt_s, q4_s, qt_s, kt_s, vt_s, k_s, v_s, gt_s, dgt_s, dqt_s, dgp_s, gated_s, dk_s, dv_s,
+    bias_s, dacc_s, dw_s, dwo_s,
 ):
-    head_of = lax.broadcasted_iota(jnp.int32, (BLOCK, PROJ), 1) // HEAD_DIM
-    masks = [(head_of == h) for h in range(HEADS)]
+    for n, ref in enumerate((wq_ref, wk_ref, wv_ref, wg_ref)):
+        wt_s[n * PROJ : (n + 1) * PROJ, :] = ref[...].astype(F32).T.astype(BF)
+    dw_s[...] = jnp.zeros_like(dw_s)
+    dwo_s[...] = jnp.zeros_like(dwo_s)
+
+    @pl.loop(0, QBLOCKS)
+    def _(b):
+        for h in range(HEADS):
+            bias_s[b, :, h * BLOCK : (h + 1) * BLOCK] = bias_ref[b, h].astype(F32).T
 
     @pl.loop(0, COL_WIDTH)
     def _(w):
-        proj = mm(act_ref[w], w_ref[...])
-        q_s[w] = (proj[:, :PROJ] * SCALE).astype(BF)
-        k_s[w] = proj[:, PROJ : 2 * PROJ].astype(BF)
-        v_s[w] = proj[:, 2 * PROJ : 3 * PROJ].astype(BF)
-        g_s[w] = jax.nn.sigmoid(proj[:, 3 * PROJ :])
-        dg_s[w] = mm(grad_ref[w], wo_ref[...], NT)
-        dkt_s[w] = jnp.zeros((PROJ, TOKENS), F32)
-        dvt_s[w] = jnp.zeros((PROJ, TOKENS), F32)
-
-    dw_s[...] = jnp.zeros_like(dw_s)
-    dwo_s[...] = jnp.zeros_like(dwo_s)
-
-    @pl.loop(0, QBLOCKS * COL_WIDTH)
-    def _(t):
-        b, w = t // COL_WIDTH, lax.rem(t, COL_WIDTH)
-        rows = pl.ds(pl.multiple_of(b * BLOCK, BLOCK), BLOCK)
-        kbs = [pl.multiple_of(kb_ref[b, s] * BLOCK, BLOCK) for s in range(SLOTS)]
-        q = q_s[w, rows, :]
-        ks = [k_s[w, pl.ds(kb, BLOCK), :] for kb in kbs]
-        vs = [v_s[w, pl.ds(kb, BLOCK), :] for kb in kbs]
-        zero = jnp.zeros((BLOCK, PROJ), BF)
-        one = jnp.ones((BLOCK, PROJ), BF)
-        k4 = jnp.concatenate([jnp.where(m, x, zero) for m in masks for x in ks], axis=0)
-        v4 = jnp.concatenate([jnp.where(m, x, zero) for m in masks for x in vs], axis=0)
-        m4 = jnp.concatenate([jnp.where(m, one, zero) for m in masks for _ in vs], axis=0)
-        vm4 = jnp.concatenate([v4, m4], axis=1)
-        scores = mm(q, k4, NT) + bias_ref[rows, :].astype(F32)
-        es = []
+        project(act_ref, grad_ref, wk_ref, wv_ref, wo_ref, wt_s, q4_s, qt_s, kt_s, vt_s, k_s, v_s,
+                gt_s, dgt_s, w)
+
+    @pl.loop(0, QBLOCKS)
+    def _(b):
+        kbs = [kb_ref[b, s] for s in range(SLOTS)]
+        dacc_s[...] = jnp.zeros_like(dacc_s)
+
+        @pl.loop(0, COL_WIDTH // UNROLL)
+        def _(t):
+            for u in range(UNROLL):
+                one_pair(kbs, bias_s, q4_s, qt_s, kt_s, vt_s, k_s, v_s, gt_s, dgt_s, dqt_s, dgp_s,
+                         gated_s, dk_s, dv_s, dacc_s, t * UNROLL + u, b)
+
         for h in range(HEADS):
-            sh = scores[:, h * WIDE : (h + 1) * WIDE]
-            es.append(jnp.exp(sh - jnp.max(sh, axis=1, keepdims=True)))
-        e = jnp.concatenate(es, axis=1)
-        e_low = e.astype(BF)
-        both = mm(e_low, vm4)
-        inv = 1.0 / both[:, PROJ:]
-        att = both[:, :PROJ] * inv
-        g = g_s[w, rows, :]
-        dg = dg_s[w, rows, :]
-        gated_s[w, rows, :] = (g * att).astype(BF)
-        datt = dg * g
-        dgp_s[w, rows, :] = (datt * att * (1.0 - g)).astype(BF)
-        datt_n = (datt * inv).astype(BF)
-        prod = datt_n.astype(F32) * att
-        dp = mm(datt_n, v4, NT)
-        dss = []
-        for h in range(HEADS):
-            delta = jnp.sum(jnp.where(masks[h], prod, 0.0), axis=1, keepdims=True)
-            dss.append(es[h] * (dp[:, h * WIDE : (h + 1) * WIDE] - delta))
-        ds = jnp.concatenate(dss, axis=1)
-        ds_low = ds.astype(BF)
-
-        @pl.when(w == 0)
-        def _():
-            dacc_s[...] = ds
-
-        @pl.when((w > 0) & (w < COL_WIDTH - 1))
-        def _():
-            dacc_s[...] += ds
-
-        @pl.when(w == COL_WIDTH - 1)
-        def _():
-            dbias_ref[rows, :] = (dacc_s[...] + ds).astype(BF)
-
-        dq_s[w, rows, :] = (mm(ds_low, k4) * SCALE).astype(BF)
-        qt = q.astype(F32).T.astype(BF)
-        dt = datt_n.astype(F32).T.astype(BF)
-        dk, dv = [], []
-        for h in range(HEADS):
-            hs = slice(h * HEAD_DIM, (h + 1) * HEAD_DIM)
-            ws = slice(h * WIDE, (h + 1) * WIDE)
-            dk.append(mm(qt[hs], ds_low[:, ws]))
-            dv.append(mm(dt[hs], e_low[:, ws]))
-        dk = jnp.concatenate(dk, axis=0)
-        dv = jnp.concatenate(dv, axis=0)
-        for s in range(SLOTS):
-            lanes = pl.ds(kbs[s], BLOCK)
-            dkt_s[w, :, lanes] += dk[:, s * BLOCK : (s + 1) * BLOCK]
-            dvt_s[w, :, lanes] += dv[:, s * BLOCK : (s + 1) * BLOCK]
+            dbias_ref[b, h] = dacc_s[:, h * BLOCK : (h + 1) * BLOCK].T.astype(BF)
 
     @pl.loop(0, COL_WIDTH)
     def _(w):
-        dk = dkt_s[w].T.astype(BF)
-        dv = dvt_s[w].T.astype(BF)
-        grads = jnp.concatenate([dq_s[w], dk, dv, dgp_s[w]], axis=1)
-        dpair_ref[w] = mm(grads, w_ref[...], NT).astype(BF)
-        xt = act_ref[w].astype(F32).T.astype(BF)
-        dw_s[...] += mm(xt, grads)
-        gt = gated_s[w].astype(F32).T.astype(BF)
-        dwo_s[...] += mm(gt, grad_ref[w])
+        finish(kb_ref, len_ref, act_ref, grad_ref, wt_s, dqt_s, dgp_s, gated_s, dk_s, dv_s, dw_s,
+               dwo_s, dpair_ref, w)
 
     for n in range(4):
-        dw_ref[n * PROJ : (n + 1) * PROJ, :] = dw_s[:, n * PROJ : (n + 1) * PROJ].astype(BF)
+        rows = slice(n * PROJ, (n + 1) * PROJ)
+        dw_ref[rows, :] = dw_s[rows, :].T.astype(BF)
     dw_ref[4 * PROJ :, :] = dwo_s[...].astype(BF)
 
 
-def compute(key_blocks, acol, gcol, full, w_all, w_out):
+def head_rows(x):
+    head_of = lax.broadcasted_iota(jnp.int32, x.shape, 0) // HEAD_DIM
+    return jnp.concatenate(
+        [jnp.where(head_of == h, x, jnp.zeros_like(x)) for h in range(HEADS)], axis=1
+    )
+
+
+def project(act_ref, grad_ref, wk_ref, wv_ref, wo_ref, wt_s, q4_s, qt_s, kt_s, vt_s, k_s, v_s,
+            gt_s, dgt_s, w):
+    x = act_ref[w]
+    turned = mm(wt_s[...], x, NT)
+    qt = (turned[:PROJ] * SCALE).astype(BF)
+    kt = turned[PROJ : 2 * PROJ].astype(BF)
+    vt = turned[2 * PROJ : 3 * PROJ].astype(BF)
+    for b in range(QBLOCKS):
+        cols = slice(b * BLOCK, (b + 1) * BLOCK)
+        qt_s[w, b] = qt[:, cols]
+        q4_s[w, b] = head_rows(qt[:, cols])
+        kt_s[w, b] = kt[:, cols]
+        vt_s[w, b] = vt[:, cols]
+        gt_s[w, b] = jax.nn.sigmoid(turned[3 * PROJ :, cols])
+    dgt = mm(wo_ref[...], grad_ref[w], NT)
+    k = mm(x, wk_ref[...]).astype(BF)
+    v = mm(x, wv_ref[...]).astype(BF)
+    for b in range(QBLOCKS):
+        rows = slice(b * BLOCK, (b + 1) * BLOCK)
+        dgt_s[w, b] = dgt[:, rows]
+        k_s[w, b] = k[rows]
+        v_s[w, b] = v[rows]
+
+
+def one_pair(kbs, bias_s, q4_s, qt_s, kt_s, vt_s, k_s, v_s, gt_s, dgt_s, dqt_s, dgp_s, gated_s,
+             dk_s, dv_s, dacc_s, w, b):
+    def chosen(ref, axis):
+        return jnp.concatenate([ref[w, kb] for kb in kbs], axis=axis)
+
+    heads = [slice(h * BLOCK, (h + 1) * BLOCK) for h in range(HEADS)]
+    scores = mm(chosen(k_s, 0), q4_s[w, b]) + bias_s[b]
+    e = jnp.exp(scores - jnp.max(scores, axis=0, keepdims=True))
+    e_low = e.astype(BF)
+    vt = chosen(vt_s, 1)
+    ones = jnp.ones((16, WIDE), BF)
+    atts, invs = [], []
+    for h in range(0, HEADS, 2):
+        lhs = jnp.concatenate([vt[h * HEAD_DIM : (h + 2) * HEAD_DIM], ones], axis=0)
+        both = mm(lhs, e_low[:, h * BLOCK : (h + 2) * BLOCK])
+        inv = 1.0 / both[2 * HEAD_DIM : 2 * HEAD_DIM + 1]
+        for n in range(2):
+            part = inv[:, n * BLOCK : (n + 1) * BLOCK]
+            raw = both[n * HEAD_DIM : (n + 1) * HEAD_DIM, n * BLOCK : (n + 1) * BLOCK]
+            atts.append(raw * part)
+            invs.append(jnp.broadcast_to(part, (HEAD_DIM, BLOCK)))
+    att = jnp.concatenate(atts, axis=0)
+    inv = jnp.concatenate(invs, axis=0)
+    g = gt_s[w, b]
+    datt = dgt_s[w, b] * g
+    gated_s[w, b] = (g * att).astype(BF)
+    dgp_s[w, b] = (datt * att * (1.0 - g)).astype(BF)
+    dn = (datt * inv).astype(BF)
+    prod = dn.astype(F32) * att
+    delta = jnp.concatenate(
+        [
+            jnp.sum(prod[h * HEAD_DIM : (h + 1) * HEAD_DIM], axis=0, keepdims=True)
+            for h in range(HEADS)
+        ],
+        axis=1,
+    )
+    ds = e * (mm(chosen(v_s, 0), head_rows(dn)) - delta)
+    dacc_s[...] += ds
+    ds_low = ds.astype(BF)
+    kt = chosen(kt_s, 1)
+    qt = qt_s[w, b]
+    for h in range(HEADS):
+        hs = slice(h * HEAD_DIM, (h + 1) * HEAD_DIM)
+        dqt_s[w, b, hs, :] = (mm(kt[hs], ds_low[:, heads[h]]) * SCALE).astype(BF)
+        dk = mm(qt[hs], ds_low[:, heads[h]], NT)
+        dv = mm(dn[hs], e_low[:, heads[h]], NT)
+        for s in range(SLOTS):
+            dk_s[w, b, s, hs, :] = dk[:, s * BLOCK : (s + 1) * BLOCK]
+            dv_s[w, b, s, hs, :] = dv[:, s * BLOCK : (s + 1) * BLOCK]
+
+
+def finish(kb_ref, len_ref, act_ref, grad_ref, wt_s, dqt_s, dgp_s, gated_s, dk_s, dv_s, dw_s, dwo_s,
+           dpair_ref, w):
+    dks, dvs = [], []
+    for k in range(QBLOCKS):
+        dk = jnp.zeros((PROJ, BLOCK), F32)
+        dv = jnp.zeros((PROJ, BLOCK), F32)
+        for b in range(QBLOCKS):
+            slot = jnp.int32(SLOTS)
+            for s in range(SLOTS):
+                slot = jnp.where((kb_ref[b, s] == k) & (s < len_ref[b]), s, slot)
+            listed = slot < SLOTS
+            at = jnp.minimum(slot, SLOTS - 1)
+            dk = dk + jnp.where(listed, dk_s[w, b, at], 0.0)
+            dv = dv + jnp.where(listed, dv_s[w, b, at], 0.0)
+        dks.append(dk.astype(BF))
+        dvs.append(dv.astype(BF))
+    parts = [
+        jnp.concatenate([dqt_s[w, b] for b in range(QBLOCKS)], axis=1),
+        jnp.concatenate(dks, axis=1),
+        jnp.concatenate(dvs, axis=1),
+        jnp.concatenate([dgp_s[w, b] for b in range(QBLOCKS)], axis=1),
+    ]
+    grads = jnp.concatenate(parts, axis=0)
+    dw_s[...] += mm(grads, act_ref[w])
+    gated = jnp.concatenate([gated_s[w, b] for b in range(QBLOCKS)], axis=1)
+    dwo_s[...] += mm(gated, grad_ref[w])
+    dpair_ref[w] = lax.dot_general(
+        grads, wt_s[...], (((0,), (0,)), ((), ())), preferred_element_type=F32
+    ).astype(BF)
+
+
+def compute(key_blocks, list_len, acol, gcol, full, *weights):
     smem = pl.BlockSpec(memory_space=pltpu.SMEM)
     vmem = pl.BlockSpec(memory_space=pltpu.VMEM)
     cols = (COL_WIDTH, TOKENS, PROJ)
+    tiles = (COL_WIDTH, QBLOCKS, PROJ, BLOCK)
+    slots = (COL_WIDTH, QBLOCKS, SLOTS, PROJ, BLOCK)
     return pl.pallas_call(
         main_kernel,
         out_shape=(
             jax.ShapeDtypeStruct(cols, BF),
-            jax.ShapeDtypeStruct((TOKENS, ALL), BF),
+            jax.ShapeDtypeStruct((QBLOCKS, HEADS, BLOCK, WIDE), BF),
             jax.ShapeDtypeStruct((WROWS, PROJ), BF),
         ),
-        in_specs=[smem] + [vmem] * 5,
+        in_specs=[smem] * 2 + [vmem] * 8,
         out_specs=(vmem, vmem, vmem),
         scratch_shapes=[
-            pltpu.VMEM(cols, BF), pltpu.VMEM(cols, BF), pltpu.VMEM(cols, BF),
-            pltpu.VMEM(cols, F32), pltpu.VMEM(cols, F32),
-            pltpu.VMEM(cols, BF), pltpu.VMEM(cols, BF), pltpu.VMEM(cols, BF),
-            pltpu.VMEM((COL_WIDTH, PROJ, TOKENS), F32), pltpu.VMEM((COL_WIDTH, PROJ, TOKENS), F32),
-            pltpu.VMEM((BLOCK, ALL), F32),
-            pltpu.VMEM((PROJ, 4 * PROJ), F32), pltpu.VMEM((PROJ, PROJ), F32),
+            pltpu.VMEM((4 * PROJ, PROJ), BF),
+            pltpu.VMEM((COL_WIDTH, QBLOCKS, PROJ, HEADS * BLOCK), BF),
+            pltpu.VMEM(tiles, BF), pltpu.VMEM(tiles, BF), pltpu.VMEM(tiles, BF),
+            pltpu.VMEM(tiles, BF), pltpu.VMEM(tiles, BF),
+            pltpu.VMEM(tiles, F32), pltpu.VMEM(tiles, F32),
+            pltpu.VMEM(tiles, BF), pltpu.VMEM(tiles, BF), pltpu.VMEM(tiles, BF),
+            pltpu.VMEM(slots, F32), pltpu.VMEM(slots, F32),
+            pltpu.VMEM((QBLOCKS, WIDE, HEADS * BLOCK), F32),
+            pltpu.VMEM((WIDE, HEADS * BLOCK), F32),
+            pltpu.VMEM((4 * PROJ, PROJ), F32), pltpu.VMEM((PROJ, PROJ), F32),
         ],
         name="attend_back",
-    )(key_blocks, acol, gcol, full, w_all, w_out)
+    )(key_blocks, list_len, acol, gcol, full, *weights)
 
 
 def out_kernel(
@@ -330,11 +389,16 @@
     y, zh, core = c // 4, lax.rem(c // 2, 2), lax.rem(c, 2)
     greet(r, c, COL_OFFS)
     sib = col_peer(c, (0, 0, 1))
+
+    def piece(cc):
+        at = pl.multiple_of(lax.rem(cc, 4) * TILE_COLS, TILE_COLS)
+        return part_ref.at[cc // 4, :, pl.ds(at, TILE_COLS), :]
+
     c1 = []
     for n in range(8):
         yy = lax.rem(y + 1 + n // 2, 4)
         cc = yy * 4 + (n % 2) * 2
-        src = part_ref.at[pl.ds((cc + 1 - core) * TILE_COLS, TILE_COLS), :]
+        src = piece(cc + 1 - core)
         cp = remote(src, r1.at[n], a1.at[n], b1.at[n], r, sib)
         cp.start()
         c1.append(cp)
@@ -361,7 +425,7 @@
         c1[n].wait_recv()
         yy = lax.rem(y + 1 + n // 2, 4)
         cc = yy * 4 + (n % 2) * 2 + core
-        own = part_ref[pl.ds(cc * TILE_COLS, TILE_COLS), :]
+        own = piece(cc)[...]
         s1[n] = (own.astype(F32) + r1[n].astype(F32)).astype(BF)
         if n < 6 and n % 2 == 1:
             m = n // 2
@@ -412,9 +476,7 @@
     acc = acc + r3[...].astype(F32)
     turned = []
     for s in range(SLOTS):
-        tile = jnp.concatenate(
-            [acc[:, h * WIDE + s * BLOCK : h * WIDE + (s + 1) * BLOCK] for h in range(HEADS)], axis=0
-        )
+        tile = acc[:, :, s * BLOCK : (s + 1) * BLOCK].reshape(PROJ, BLOCK)
         turned.append(tile.T)
     for k in range(QBLOCKS):
         val = jnp.zeros((BLOCK, PROJ), F32)
@@ -445,7 +507,7 @@
     smem = pl.BlockSpec(memory_space=pltpu.SMEM)
     vmem = pl.BlockSpec(memory_space=pltpu.VMEM)
     dma = pltpu.SemaphoreType.DMA
-    piece = (TILE_COLS, ALL)
+    piece = (HEADS, TILE_COLS, WIDE)
     return pl.pallas_call(
         out_kernel,
         out_shape=(
@@ -476,9 +538,10 @@
     act = jnp.transpose(pair_act, (1, 0, 2))
     grad = jnp.transpose(out_grad, (1, 0, 2))
     bias = jnp.transpose(tri_bias, (1, 0, 2)).reshape(TILE_ROWS, PROJ)
-    w_all = jnp.concatenate([w_query, w_key, w_value, w_gate], axis=1)
     acol, gcol, full = gather_in(key_blocks, list_len, act, grad, bias)
-    dpair, part, dw = compute(key_blocks, acol, gcol, full, w_all, w_out)
+    dpair, part, dw = compute(
+        key_blocks, list_len, acol, gcol, full, w_query, w_key, w_value, w_gate, w_out
+    )
     dp, db, ws = send_out(key_blocks, list_len, dpair, part, dw)
     d_pair = jnp.transpose(dp, (1, 0, 2))
     d_bias = jnp.transpose(db.reshape(TILE_ROWS, HEADS, TILE_COLS), (1, 0, 2))

time: 105 us -> 104 us (level)
  other arithmetic: 1.48 us -> 0 us
    concatenate x1 -> x0, other arithmetic: 1.48 us -> none  [on_device(): w_all = jnp.concatenate([w_query, w_key, w_value, w_gate], axis=1)]
where the time goes in v2:
time: 104 us; the launch traced here: 103 us
  Pallas kernels  93.4 us (90%)
  local copies, waits for them, and re-layouts  9.37 us (9%)
    pallas_call x1, Pallas kernels, send_out(): pl.pallas_call(out_kernel, out_shape=(jax.ShapeDtypeStruct((TILE_COLS, TI...  37.5 us
    pallas_call x1, Pallas kernels, compute(): pl.pallas_call(main_kernel, out_shape=(jax.ShapeDtypeStruct(cols, BF), ja...  28.7 us
    pallas_call x1, Pallas kernels, gather_in(): pl.pallas_call(in_kernel, out_shape=(jax.ShapeDtypeStruct((COL_WIDTH, TOK...  27.2 us
    transpose x1, local copies, waits for them, and re-layouts, on_device(): grad = jnp.transpose(out_grad, (1, 0, 2))  2.57 us
    unnamed x1, local copies, waits for them, and re-layouts  2.18 us

profile of v2, /device:TPU:1, one launch (start us, length us, event | category | flops | bytes accessed | tf_op | source)
XLA Modules:
  0.0 103.4 jit_solution(6194423031418720901)
XLA Ops:
  0.6 1.4 %copy.24.bias_ref = bf16[64,128]{1,0:T(8,128)(2,1)} copy(bf16[64,128]{0,1:T(8,128)(2,1)} %bitcast.13) | data formatting | bytes 32768 | tf_op jit(solution)/shard_map/reshape | solution.py:540
  2.1 2.6 %copy_bitcast_fusion = (bf16[32,64,128]{2,1,0:T(8,128)(2,1)}, bf16[32,64,128]{2,1,0:T(8,128)(2,1)}) fusion(bf16[64,32,128]{2,1,0:T(8,128)(2,1)} %param.11, bf16[64,32,128]{2,1,0:T(8,128)(2,1)} %param.10), kind=kLoop, calls=%fused_computation | loop fusion | bytes 2097152 | tf_op jit(solution)/shard_map/transpose | solution.py:539
  4.7 27.2 %gather_in.1 = (bf16[4,512,128]{2,1,0:T(8,128)(2,1)}, bf16[4,512,128]{2,1,0:T(8,128)(2,1)}, bf16[4,4,128,384]{3,2,1,0:T(8,128)(2,1)}) custom-call(s32[4,3]{1,0:T(4,128)} %kb_ref.5, s32[4]{0:T(128)} %len_ref.5, bf16[32,64,128]{2,1,0:T(8,128)(2,1)} %get-tuple-element.45.act_ref, bf16[32,64,128]{2,1,0:T(8,128)(2,1)} %get-tuple-element.44.grad_ref, ...), custom_call_target="tpu_custom_call" | custom-call | tf_op jit(solution)/shard_map/gather_in/pallas_call | solution.py:163
  31.8 28.7 %attend_back.1 = (bf16[4,512,128]{2,1,0:T(8,128)(2,1)}, bf16[4,4,128,384]{3,2,1,0:T(8,128)(2,1)}, bf16[640,128]{1,0:T(8,128)(2,1)}) custom-call(s32[4,3]{1,0:T(4,128)} %kb_ref.5, s32[4]{0:T(128)} %len_ref.5, bf16[4,512,128]{2,1,0:T(8,128)(2,1)} %get-tuple-element.16.act_ref, bf16[4,512,128]{2,1,0:T(8,128)(2,1)} %get-tuple-element.17.grad_ref, ...), custom_call_target="tpu_custom_call" | custom-call | tf_op jit(solution)/shard_map/attend_back/pallas_call | solution.py:358
  60.6 37.5 %send_out.1 = (bf16[32,64,128]{2,1,0:T(8,128)(2,1)}, f32[64,128]{1,0:T(8,128)}, f32[640,128]{1,0:T(8,128)}) custom-call(s32[4,3]{1,0:T(4,128)} %kb_ref.5, s32[4]{0:T(128)} %len_ref.5, bf16[4,512,128]{2,1,0:T(8,128)(2,1)} %get-tuple-element.19.dpair_ref, bf16[4,4,128,384]{3,2,1,0:T(8,128)(2,1)} %get-tuple-element.20.part_ref, ...), custom_call_target="tpu_custom_call" | custom-call | tf_op jit(solution)/shard_map/send_out/pallas_call | solution.py:511
  98.0 2.2 %copy.26 = bf16[64,32,128]{2,1,0:T(8,128)(2,1)} copy(bf16[64,32,128]{2,0,1:T(8,128)(2,1)} %bitcast.11) | data formatting | bytes 1048576
  100.2 1.5 %copy.25 = f32[64,128]{0,1:T(8,128)} copy(f32[64,128]{1,0:T(8,128)} %get-tuple-element.23) | data formatting | bytes 65536 | tf_op jit(solution)/shard_map/send_out/pallas_call | solution.py:511
  101.7 1.7 %fusion = (f32[128,128]{1,0:T(8,128)}, f32[128,128]{1,0:T(8,128)}, f32[128,128]{1,0:T(8,128)}, f32[128,128]{1,0:T(8,128)}, f32[128,128]{1,0:T(8,128)}) fusion(f32[640,128]{1,0:T(8,128)} %get-tuple-element.24), kind=kLoop, calls=%fused_computation.2 | loop fusion | bytes 655360 | tf_op jit(solution)/shard_map/slice | solution.py:548

commit v3 on v2

v3 whole, which is shorter than its diff:
```python
import jax
import jax.numpy as jnp
from jax import lax
from jax.experimental import pallas as pl
from jax.experimental.pallas import tpu as pltpu
from jax.sharding import PartitionSpec as P

BF = jnp.bfloat16
F32 = jnp.float32
HEADS = 4
HEAD_DIM = 32
PROJ = HEADS * HEAD_DIM
BLOCK = 128
QBLOCKS = 4
SLOTS = 3
TOKENS = QBLOCKS * BLOCK
WIDE = SLOTS * BLOCK
ROWS = 8
COLS = 16
TILE_ROWS = TOKENS // ROWS
TILE_COLS = TOKENS // COLS
COL_WIDTH = TILE_COLS // ROWS
WROWS = 5 * PROJ
WPART = WROWS // ROWS
DEAD = -1e30
SCALE = HEAD_DIM ** -0.5

ROW_OFFS = [(dz, dx) for dz in range(2) for dx in range(4)][1:]
COL_OFFS = [(dy, dz, dc) for dy in range(4) for dz in range(2) for dc in range(2)][1:]


def row_peer(r, off):
    z, x = r // 4, lax.rem(r, 4)
    return lax.rem(z + off[0], 2) * 4 + lax.rem(x + off[1], 4)


def col_peer(c, off):
    y, z, k = c // 4, lax.rem(c // 2, 2), lax.rem(c, 2)
    return lax.rem(y + off[0], 4) * 4 + lax.rem(z + off[1], 2) * 2 + lax.rem(k + off[2], 2)


def remote(src, dst, ssem, rsem, r, c):
    return pltpu.make_async_remote_copy(
        src_ref=src,
        dst_ref=dst,
        send_sem=ssem,
        recv_sem=rsem,
        device_id=(r, c),
        device_id_type=pl.DeviceIdType.MESH,
    )


NT = (((1,), (1,)), ((), ()))
NN = (((1,), (0,)), ((), ()))


def mm(a, b, dims=NN):
    return lax.dot_general(a, b, dims, preferred_element_type=F32)


def head_rows(x):
    head_of = lax.broadcasted_iota(jnp.int32, x.shape, 0) // HEAD_DIM
    return jnp.concatenate(
        [jnp.where(head_of == h, x, jnp.zeros_like(x)) for h in range(HEADS)], axis=1
    )


def project(act_ref, grad_ref, wk_ref, wv_ref, wo_ref, wt_s, q4_s, qt_s, kt_s, vt_s, k_s, v_s,
            gt_s, dgt_s, w):
    x = act_ref[w]
    turned = mm(wt_s[...], x, NT)
    qt = (turned[:PROJ] * SCALE).astype(BF)
    kt = turned[PROJ : 2 * PROJ].astype(BF)
    vt = turned[2 * PROJ : 3 * PROJ].astype(BF)
    for b in range(QBLOCKS):
        cols = slice(b * BLOCK, (b + 1) * BLOCK)
        qt_s[w, b] = qt[:, cols]
        q4_s[w, b] = head_rows(qt[:, cols])
        kt_s[w, b] = kt[:, cols]
        vt_s[w, b] = vt[:, cols]
        gt_s[w, b] = jax.nn.sigmoid(turned[3 * PROJ :, cols])
    dgt = mm(wo_ref[...], grad_ref[w], NT)
    k = mm(x, wk_ref[...]).astype(BF)
    v = mm(x, wv_ref[...]).astype(BF)
    for b in range(QBLOCKS):
        rows = slice(b * BLOCK, (b + 1) * BLOCK)
        dgt_s[w, b] = dgt[:, rows]
        k_s[w, b] = k[rows]
        v_s[w, b] = v[rows]


def one_pair(kbs, bias_s, q4_s, qt_s, kt_s, vt_s, k_s, v_s, gt_s, dgt_s, dqt_s, dgp_s, gated_s,
             dk_s, dv_s, dacc_s, w, b):
    def chosen(ref, axis):
        return jnp.concatenate([ref[w, kb] for kb in kbs], axis=axis)

    heads = [slice(h * BLOCK, (h + 1) * BLOCK) for h in range(HEADS)]
    scores = mm(chosen(k_s, 0), q4_s[w, b]) + bias_s[0]
    e = jnp.exp(scores - jnp.max(scores, axis=0, keepdims=True))
    e_low = e.astype(BF)
    vt = chosen(vt_s, 1)
    ones = jnp.ones((16, WIDE), BF)
    atts, invs = [], []
    for h in range(0, HEADS, 2):
        lhs = jnp.concatenate([vt[h * HEAD_DIM : (h + 2) * HEAD_DIM], ones], axis=0)
        both = mm(lhs, e_low[:, h * BLOCK : (h + 2) * BLOCK])
        inv = 1.0 / both[2 * HEAD_DIM : 2 * HEAD_DIM + 1]
        for n in range(2):
            part = inv[:, n * BLOCK : (n + 1) * BLOCK]
            raw = both[n * HEAD_DIM : (n + 1) * HEAD_DIM, n * BLOCK : (n + 1) * BLOCK]
            atts.append(raw * part)
            invs.append(jnp.broadcast_to(part, (HEAD_DIM, BLOCK)))
    att = jnp.concatenate(atts, axis=0)
    inv = jnp.concatenate(invs, axis=0)
    g = gt_s[w, b]
    datt = dgt_s[w, b] * g
    gated_s[w, b] = (g * att).astype(BF)
    dgp_s[w, b] = (datt * att * (1.0 - g)).astype(BF)
    dn = (datt * inv).astype(BF)
    prod = dn.astype(F32) * att
    delta = jnp.concatenate(
        [
            jnp.sum(prod[h * HEAD_DIM : (h + 1) * HEAD_DIM], axis=0, keepdims=True)
            for h in range(HEADS)
        ],
        axis=1,
    )
    ds = e * (mm(chosen(v_s, 0), head_rows(dn)) - delta)
    dacc_s[...] += ds
    ds_low = ds.astype(BF)
    kt = chosen(kt_s, 1)
    qt = qt_s[w, b]
    for h in range(HEADS):
        hs = slice(h * HEAD_DIM, (h + 1) * HEAD_DIM)
        dqt_s[w, b, hs, :] = (mm(kt[hs], ds_low[:, heads[h]]) * SCALE).astype(BF)
        dk = mm(qt[hs], ds_low[:, heads[h]], NT)
        dv = mm(dn[hs], e_low[:, heads[h]], NT)
        for s in range(SLOTS):
            dk_s[w, b, s, hs, :] = dk[:, s * BLOCK : (s + 1) * BLOCK]
            dv_s[w, b, s, hs, :] = dv[:, s * BLOCK : (s + 1) * BLOCK]


def collect(kb_ref, len_ref, act_ref, grad_ref, dqt_s, dgp_s, gated_s, dk_s, dv_s, dw_s, dwo_s,
            grads_s, w):
    dks, dvs = [], []
    for k in range(QBLOCKS):
        dk = jnp.zeros((PROJ, BLOCK), F32)
        dv = jnp.zeros((PROJ, BLOCK), F32)
        for b in range(QBLOCKS):
            slot = jnp.int32(SLOTS)
            for s in range(SLOTS):
                slot = jnp.where((kb_ref[b, s] == k) & (s < len_ref[b]), s, slot)
            listed = slot < SLOTS
            at = jnp.minimum(slot, SLOTS - 1)
            dk = dk + jnp.where(listed, dk_s[w, b, at], 0.0)
            dv = dv + jnp.where(listed, dv_s[w, b, at], 0.0)
        dks.append(dk.astype(BF))
        dvs.append(dv.astype(BF))
    parts = [
        jnp.concatenate([dqt_s[w, b] for b in range(QBLOCKS)], axis=1),
        jnp.concatenate(dks, axis=1),
        jnp.concatenate(dvs, axis=1),
        jnp.concatenate([dgp_s[w, b] for b in range(QBLOCKS)], axis=1),
    ]
    grads = jnp.concatenate(parts, axis=0)
    grads_s[w] = grads
    dw_s[...] += mm(grads, act_ref[w])
    gated = jnp.concatenate([gated_s[w, b] for b in range(QBLOCKS)], axis=1)
    dwo_s[...] += mm(gated, grad_ref[w])


class Sems:
    def __init__(self, send, recv):
        self.send, self.recv, self.used = send, recv, 0

    def remote(self, src, dst, r, c):
        n = self.used
        self.used += 1
        cp = remote(src, dst, self.send.at[n], self.recv.at[n], r, c)
        cp.start()
        return cp


N_SEMS = 56 + 28 + 24 + 29 + 24


def fused_kernel(
    kb_ref, len_ref, pair_ref, cot_ref, bias_ref, wq_ref, wk_ref, wv_ref, wg_ref, wo_ref,
    dp_ref, db_ref, wsum_ref,
    flat_s, actt, gradt, act_s, grad_s, turned, got, mine, full,
    wt_s, q4_s, qt_s, kt_s, vt_s, k_s, v_s, gt_s, dgt_s, dqt_s, dgp_s, gated_s, dk_s, dv_s,
    bias_s, dacc_s, dw_s, dwo_s, grads_s, dpair_s,
    part, r1, s1, r2, s2, r3, dense, r4, dwb, r5, s6, w6,
    send_sem, recv_sem,
):
    r, c = lax.axis_index("row"), lax.axis_index("col")
    y, zh, core = c // 4, lax.rem(c // 2, 2), lax.rem(c, 2)
    sems = Sems(send_sem, recv_sem)
    barrier = pltpu.get_barrier_semaphore()
    peers = [(row_peer(r, off), c) for off in ROW_OFFS] + [(r, col_peer(c, o)) for o in COL_OFFS]
    for peer in peers:
        pl.semaphore_signal(barrier, inc=1, device_id=peer, device_id_type=pl.DeviceIdType.MESH)

    turned[...] = bias_ref[...].astype(F32).T.astype(BF)
    for src, dst in ((pair_ref, actt), (cot_ref, gradt)):
        flat_s[...] = src[...].astype(F32).reshape(TILE_ROWS * TILE_COLS, PROJ)

        @pl.loop(0, TILE_COLS // 4)
        def _(n):
            for u in range(4):
                j = n * 4 + u
                dst[j] = flat_s[pl.ds(j, TILE_ROWS, stride=TILE_COLS), :].astype(BF)

    got[r] = turned[...]
    pl.semaphore_wait(barrier, len(peers))

    first = [sems.remote(turned, got.at[r], row_peer(r, off), c) for off in ROW_OFFS]
    rows = pl.ds(pl.multiple_of(r * TILE_ROWS, TILE_ROWS), TILE_ROWS)
    big = []
    for w in range(COL_WIDTH):
        now = []
        for off in ROW_OFFS:
            p = row_peer(r, off)
            now.append(sems.remote(actt.at[p * COL_WIDTH + w], act_s.at[w, rows, :], p, c))
            now.append(sems.remote(gradt.at[p * COL_WIDTH + w], grad_s.at[w, rows, :], p, c))
        big.append(now)
    for w in range(COL_WIDTH):
        act_s[w, rows, :] = actt[r * COL_WIDTH + w]
        grad_s[w, rows, :] = gradt[r * COL_WIDTH + w]
    for n, ref in enumerate((wq_ref, wk_ref, wv_ref, wg_ref)):
        wt_s[n * PROJ : (n + 1) * PROJ, :] = ref[...].astype(F32).T.astype(BF)
    dw_s[...] = jnp.zeros_like(dw_s)
    dwo_s[...] = jnp.zeros_like(dwo_s)

    for cp in first:
        cp.wait_recv()
    for s in range(SLOTS):
        k = kb_ref[y, s]
        tile = jnp.concatenate([got[2 * k], got[2 * k + 1]], axis=0).astype(F32)
        tile = jnp.where(s < len_ref[y], tile, DEAD).T.astype(BF)
        mine[:, :, s * BLOCK : (s + 1) * BLOCK] = tile.reshape(HEADS, TILE_COLS, BLOCK)

    def piece(ref, cc):
        at = pl.multiple_of(lax.rem(cc, 4) * TILE_COLS, TILE_COLS)
        return ref.at[cc // 4, :, pl.ds(at, TILE_COLS), :]

    zc, sib = col_peer(c, (0, 1, 0)), col_peer(c, (0, 0, 1))
    ys = [col_peer(c, (n + 1, 0, 0)) for n in range(3)]
    cz = sems.remote(mine, piece(full, c), r, zc)
    to_y = [sems.remote(mine, piece(full, c), r, ys[n]) for n in range(3)]
    cs = sems.remote(mine, piece(full, c), r, sib)
    piece(full, c)[...] = mine[...]
    cz.wait_recv()
    to_y += [sems.remote(piece(full, zc), piece(full, zc), r, ys[n]) for n in range(3)]
    fwd = [sems.remote(piece(full, zc), piece(full, zc), r, sib)]

    def column(w):
        for cp in big[w]:
            cp.wait_recv()
        project(act_s, grad_s, wk_ref, wv_ref, wo_ref, wt_s, q4_s, qt_s, kt_s, vt_s, k_s, v_s,
                gt_s, dgt_s, w)

    def pass_on(z):
        for n in range(3):
            to_y[3 * z + n].wait_recv()
            cc = col_peer(c, (3 - n, z, 0))
            fwd.append(sems.remote(piece(full, cc), piece(full, cc), r, sib))

    column(0)
    pass_on(0)
    column(1)
    pass_on(1)
    column(2)
    column(3)
    cs.wait_recv()
    for cp in fwd:
        cp.wait_recv()

    c1, c2 = [], []
    total = None

    def merge(t):
        for n in range(2):
            c1[t][n].wait_recv()
            at = pl.multiple_of((2 * n + core) * TILE_COLS, TILE_COLS)
            own = part[t, :, pl.ds(at, TILE_COLS), :]
            s1[t, n] = (own.astype(F32) + r1[t, n].astype(F32)).astype(BF)

    for t in range(QBLOCKS):
        b = lax.rem(y + 1 + t, QBLOCKS)
        kbs = [kb_ref[b, s] for s in range(SLOTS)]
        for h in range(HEADS):
            bias_s[0, :, h * BLOCK : (h + 1) * BLOCK] = full[b, h].astype(F32).T
        dacc_s[...] = jnp.zeros_like(dacc_s)

        @pl.loop(0, COL_WIDTH)
        def _(w):
            one_pair(kbs, bias_s, q4_s, qt_s, kt_s, vt_s, k_s, v_s, gt_s, dgt_s, dqt_s, dgp_s,
                     gated_s, dk_s, dv_s, dacc_s, w, b)

        for h in range(HEADS):
            part[t, h] = dacc_s[:, h * BLOCK : (h + 1) * BLOCK].T.astype(BF)
        now = []
        for n in range(2):
            at = pl.multiple_of((2 * n + 1 - core) * TILE_COLS, TILE_COLS)
            now.append(sems.remote(part.at[t, :, pl.ds(at, TILE_COLS), :], r1.at[t, n], r, sib))
        c1.append(now)
        if t > 0:
            merge(t - 1)
            c2.append(sems.remote(s1.at[t - 1], r2.at[t - 1], r, ys[t - 1]))

    @pl.loop(0, COL_WIDTH)
    def _(w):
        collect(kb_ref, len_ref, act_s, grad_s, dqt_s, dgp_s, gated_s, dk_s, dv_s, dw_s, dwo_s,
                grads_s, w)

    for n in range(4):
        at = slice(n * PROJ, (n + 1) * PROJ)
        dwb[at, :] = dw_s[at, :].T.astype(BF)
    dwb[4 * PROJ :, :] = dwo_s[...].astype(BF)
    c5 = []
    for n, off in enumerate(ROW_OFFS):
        p = row_peer(r, off)
        src = dwb.at[pl.ds(pl.multiple_of(p * WPART, 16), WPART), :]
        c5.append(sems.remote(src, r5.at[n], p, c))
    merge(3)
    for cp in c2:
        cp.wait_recv()

    def share(z):
        acc = s1[3, z].astype(F32)
        for m in range(3):
            acc = acc + r2[m, z].astype(F32)
        return acc

    s2[...] = share(1 - zh).astype(BF)
    c3 = sems.remote(s2, r3, r, zc)
    cd = []
    w_all = jnp.concatenate([ref[...] for ref in (wq_ref, wk_ref, wv_ref, wg_ref)], axis=1)
    for w in range(COL_WIDTH):
        back = mm(w_all, grads_s[w])
        for b in range(QBLOCKS):
            at = slice(b * BLOCK, (b + 1) * BLOCK)
            dpair_s[w, at, :] = back[:, at].T.astype(BF)
        for off in ROW_OFFS:
            p = row_peer(r, off)
            src = dpair_s.at[w, pl.ds(pl.multiple_of(p * TILE_ROWS, TILE_ROWS), TILE_ROWS), :]
            cd.append(sems.remote(src, dp_ref.at[r * COL_WIDTH + w], p, c))
        if w == 1:
            for cp in c5:
                cp.wait_recv()
            tot = dwb[pl.ds(pl.multiple_of(r * WPART, 16), WPART), :].astype(F32)
            for n in range(7):
                tot = tot + r5[n].astype(F32)
            s6[...] = tot.astype(BF)
            w6[c] = s6[...]
            c6 = [sems.remote(s6, w6.at[c], r, col_peer(c, off)) for off in COL_OFFS]
    for w in range(COL_WIDTH):
        dp_ref[r * COL_WIDTH + w] = dpair_s[w, rows, :]
    acc = share(zh)
    c3.wait_recv()
    acc = acc + r3[...].astype(F32)
    tiles = [
        acc[:, :, s * BLOCK : (s + 1) * BLOCK].reshape(PROJ, BLOCK).T for s in range(SLOTS)
    ]
    for k in range(QBLOCKS):
        val = jnp.zeros((BLOCK, PROJ), F32)
        for s in range(SLOTS):
            hit = (kb_ref[y, s] == k) & (s < len_ref[y])
            val = val + jnp.where(hit, tiles[s], 0.0)
        dense[k * BLOCK : (k + 1) * BLOCK, :] = val.astype(BF)
    c4 = []
    for n, off in enumerate(ROW_OFFS):
        p = row_peer(r, off)
        src = dense.at[pl.ds(pl.multiple_of(p * TILE_ROWS, TILE_ROWS), TILE_ROWS), :]
        c4.append(sems.remote(src, r4.at[n], p, c))
    for cp in c6:
        cp.wait_recv()
    tot = w6[0].astype(F32)
    for n in range(1, COLS):
        tot = tot + w6[n].astype(F32)
    myrows = pl.ds(pl.multiple_of(r * WPART, 16), WPART)
    wsum_ref[myrows, :] = tot
    c7 = [
        sems.remote(wsum_ref.at[myrows, :], wsum_ref.at[myrows, :], row_peer(r, off), c)
        for off in ROW_OFFS
    ]
    val = dense[rows, :].astype(F32)
    for n in range(7):
        c4[n].wait_recv()
        val = val + r4[n].astype(F32)
    db_ref[...] = val.T
    for cp in cd + c7:
        cp.wait_recv()
    for cp in sum(big, []) + first + [cz, cs, c3] + to_y + fwd + sum(c1, []) + c2 + c4 + c5 + c6 + c7 + cd:
        cp.wait_send()


def fused(key_blocks, list_len, act, grad, bias, *weights):
    any_ = pl.BlockSpec(memory_space=pl.ANY)
    smem = pl.BlockSpec(memory_space=pltpu.SMEM)
    vmem = pl.BlockSpec(memory_space=pltpu.VMEM)
    dma = pltpu.SemaphoreType.DMA
    flip = (TILE_COLS, TILE_ROWS, PROJ)
    cols = (COL_WIDTH, TOKENS, PROJ)
    tiles = (COL_WIDTH, QBLOCKS, PROJ, BLOCK)
    slots = (COL_WIDTH, QBLOCKS, SLOTS, PROJ, BLOCK)
    whole = (QBLOCKS, HEADS, BLOCK, WIDE)
    piece = (HEADS, TILE_COLS, WIDE)
    return pl.pallas_call(
        fused_kernel,
        out_shape=(
            jax.ShapeDtypeStruct(flip, BF),
            jax.ShapeDtypeStruct((PROJ, TILE_ROWS), F32),
            jax.ShapeDtypeStruct((WROWS, PROJ), F32),
        ),
        in_specs=[smem] * 2 + [vmem] * 8,
        out_specs=(vmem, vmem, vmem),
        scratch_shapes=[
            pltpu.VMEM((TILE_ROWS * TILE_COLS, PROJ), F32),
            pltpu.VMEM(flip, BF), pltpu.VMEM(flip, BF),
            pltpu.VMEM(cols, BF), pltpu.VMEM(cols, BF),
            pltpu.VMEM((TILE_ROWS, PROJ), BF), pltpu.VMEM((ROWS, TILE_ROWS, PROJ), BF),
            pltpu.VMEM(piece, BF), pltpu.VMEM(whole, BF),
            pltpu.VMEM((4 * PROJ, PROJ), BF),
            pltpu.VMEM((COL_WIDTH, QBLOCKS, PROJ, HEADS * BLOCK), BF),
            pltpu.VMEM(tiles, BF), pltpu.VMEM(tiles, BF), pltpu.VMEM(tiles, BF),
            pltpu.VMEM(tiles, BF), pltpu.VMEM(tiles, BF),
            pltpu.VMEM(tiles, F32), pltpu.VMEM(tiles, F32),
            pltpu.VMEM(tiles, BF), pltpu.VMEM(tiles, BF), pltpu.VMEM(tiles, BF),
            pltpu.VMEM(slots, F32), pltpu.VMEM(slots, F32),
            pltpu.VMEM((1, WIDE, HEADS * BLOCK), F32),
            pltpu.VMEM((WIDE, HEADS * BLOCK), F32),
            pltpu.VMEM((4 * PROJ, PROJ), F32), pltpu.VMEM((PROJ, PROJ), F32),
            pltpu.VMEM((COL_WIDTH, 4 * PROJ, TOKENS), BF), pltpu.VMEM(cols, BF),
            pltpu.VMEM(whole, BF), pltpu.VMEM((QBLOCKS, 2, *piece), BF),
            pltpu.VMEM((QBLOCKS, 2, *piece), BF), pltpu.VMEM((3, 2, *piece), BF),
            pltpu.VMEM(piece, BF), pltpu.VMEM(piece, BF),
            pltpu.VMEM((TOKENS, PROJ), BF), pltpu.VMEM((7, TILE_ROWS, PROJ), BF),
            pltpu.VMEM((WROWS, PROJ), BF), pltpu.VMEM((7, WPART, PROJ), BF),
            pltpu.VMEM((WPART, PROJ), BF), pltpu.VMEM((COLS, WPART, PROJ), BF),
            dma((N_SEMS,)), dma((N_SEMS,)),
        ],
        compiler_params=pltpu.CompilerParams(
            collective_id=0, has_side_effects=True, vmem_limit_bytes=60 * 1024 * 1024
        ),
        name="attend_back",
    )(key_blocks, list_len, act, grad, bias, *weights)


def on_device(
    pair_act, out_grad, tri_bias, w_query, w_key, w_value, w_gate, w_out, key_blocks, list_len
):
    bias = jnp.transpose(tri_bias, (0, 2, 1)).reshape(PROJ, TILE_ROWS)
    dp, db, ws = fused(
        key_blocks, list_len, pair_act, out_grad, bias, w_query, w_key, w_value, w_gate, w_out
    )
    d_pair = jnp.transpose(dp, (1, 0, 2))
    d_bias = jnp.transpose(db.reshape(HEADS, TILE_COLS, TILE_ROWS), (0, 2, 1))
    return (d_pair, d_bias) + tuple(ws[n * PROJ : (n + 1) * PROJ] for n in range(5))


def solution(mesh):
    in_specs = (
        P("row", "col", None), P("row", "col", None), P(None, "row", "col"),
        P(), P(), P(), P(), P(), P(), P(),
    )
    out_specs = (P("row", "col", None), P(None, "row", "col"), P(), P(), P(), P(), P())
    return jax.shard_map(
        on_device, mesh=mesh, in_specs=in_specs, out_specs=out_specs, check_vma=False
    )
```

time: 104 us -> 90.7 us (0.87)
  Pallas kernels: 93.4 us -> 86.1 us
  local copies, waits for them, and re-layouts: 9.37 us -> 3.72 us
    pallas_call x3 -> x1, Pallas kernels: 93.4 us -> 86.1 us  [fused(): pl.pallas_call(fused_kernel, out_shape=(jax.ShapeDtypeStruct(flip, BF), j...]
    transpose x1 -> x0, local copies, waits for them, and re-layouts: 2.57 us -> none  [on_device(): grad = jnp.transpose(out_grad, (1, 0, 2))]
    pallas_call x1 -> x0, local copies, waits for them, and re-layouts: 1.49 us -> none  [send_out(): pl.pallas_call(out_kernel, out_shape=(jax.ShapeDtypeStruct((TILE_COLS, TI...]
    reshape x1 -> x0, local copies, waits for them, and re-layouts: 1.45 us -> none  [on_device(): bias = jnp.transpose(tri_bias, (1, 0, 2)).reshape(TILE_ROWS, PROJ)]
    unnamed x1 -> x6, local copies, waits for them, and re-layouts: 2.18 us -> 3 us
where the time goes in v3:
time: 90.7 us; the launch traced here: 90.5 us
  Pallas kernels  86.1 us (95%)
  local copies, waits for them, and re-layouts  3.72 us (4%)
    pallas_call x1, Pallas kernels, fused(): pl.pallas_call(fused_kernel, out_shape=(jax.ShapeDtypeStruct(flip, BF), j...  86.1 us
    unnamed x6, local copies, waits for them, and re-layouts  3 us

profile of v3, /device:TPU:1, one launch (start us, length us, event | category | flops | bytes accessed | tf_op | source)
XLA Modules:
  0.0 90.5 jit_solution(5601503448035065960)
XLA Ops:
  0.6 86.1 %attend_back.1 = (bf16[32,64,128]{2,1,0:T(8,128)(2,1)}, f32[128,64]{1,0:T(8,128)}, f32[640,128]{1,0:T(8,128)}) custom-call(s32[4,3]{1,0:T(4,128)} %kb_ref.1, s32[4]{0:T(128)} %len_ref.1, bf16[64,32,128]{2,1,0:T(8,128)(2,1)} %pair_ref.1, bf16[64,32,128]{2,1,0:T(8,128)(2,1)} %cot_ref.1, bf16[128,64]{1,0:T(8,128)(2,1)} %bitcast.9, bf16[128,128]{1,0:T(8,128)(2,1)} %wq_ref.1, ...), custom_call_target="tpu_custom_call" | custom-call | tf_op jit(solution)/shard_map/attend_back/pallas_call | solution.py:410
  86.7 0.0 copy-start
  86.7 2.2 %copy.17 = bf16[64,32,128]{2,1,0:T(8,128)(2,1)} copy(bf16[64,32,128]{2,0,1:T(8,128)(2,1)} %bitcast.7) | data formatting | bytes 1048576
  89.0 0.0 copy-done
  89.0 0.0 copy-start.1
  89.0 0.7 fusion
  89.7 0.1 copy-done.1
  89.8 0.6 copy.19
Async XLA Ops:
  86.7 2.2 %copy-start = (f32[640,128]{1,0:T(8,128)S(1)}, f32[640,128]{1,0:T(8,128)}, u32[]{:S(2)}) copy-start(f32[640,128]{1,0:T(8,128)} %get-tuple-element.12) | copy-start | bytes 983044
  89.0 0.9 copy-start.1

commit v4 on v3

--- a/solution.py
+++ b/solution.py
@@ -21,12 +21,16 @@
 TILE_COLS = TOKENS // COLS
 COL_WIDTH = TILE_COLS // ROWS
 WROWS = 5 * PROJ
-WPART = WROWS // ROWS
+PLANE = 16
+PILLAR = 8
+WPART = 48
+WPAD = WPART * PLANE
 DEAD = -1e30
 SCALE = HEAD_DIM ** -0.5
 
 ROW_OFFS = [(dz, dx) for dz in range(2) for dx in range(4)][1:]
-COL_OFFS = [(dy, dz, dc) for dy in range(4) for dz in range(2) for dc in range(2)][1:]
+PLANE_OFFS = [(dz, dx, dh) for dh in range(2) for dz in range(2) for dx in range(4)][1:]
+PILLAR_OFFS = [(dy, 0, dc) for dy in range(4) for dc in range(2)][1:]
 
 
 def row_peer(r, off):
@@ -95,7 +99,7 @@
         return jnp.concatenate([ref[w, kb] for kb in kbs], axis=axis)
 
     heads = [slice(h * BLOCK, (h + 1) * BLOCK) for h in range(HEADS)]
-    scores = mm(chosen(k_s, 0), q4_s[w, b]) + bias_s[0]
+    scores = mm(chosen(k_s, 0), q4_s[w, b]) + bias_s[b]
     e = jnp.exp(scores - jnp.max(scores, axis=0, keepdims=True))
     e_low = e.astype(BF)
     vt = chosen(vt_s, 1)
@@ -126,7 +130,7 @@
         axis=1,
     )
     ds = e * (mm(chosen(v_s, 0), head_rows(dn)) - delta)
-    dacc_s[...] += ds
+    dacc_s[b] += ds
     ds_low = ds.astype(BF)
     kt = chosen(kt_s, 1)
     qt = qt_s[w, b]
@@ -173,15 +177,18 @@
     def __init__(self, send, recv):
         self.send, self.recv, self.used = send, recv, 0
 
-    def remote(self, src, dst, r, c):
+    def later(self, src, dst, r, c):
         n = self.used
         self.used += 1
-        cp = remote(src, dst, self.send.at[n], self.recv.at[n], r, c)
+        return remote(src, dst, self.send.at[n], self.recv.at[n], r, c)
+
+    def remote(self, src, dst, r, c):
+        cp = self.later(src, dst, r, c)
         cp.start()
         return cp
 
 
-N_SEMS = 56 + 28 + 24 + 29 + 24
+N_SEMS = 15 + 56 + 6 + 2 + 6 + 28 + 8 + 3 + 15 + 15 + 7 + 15
 
 
 def fused_kernel(
@@ -190,14 +197,20 @@
     flat_s, actt, gradt, act_s, grad_s, turned, got, mine, full,
     wt_s, q4_s, qt_s, kt_s, vt_s, k_s, v_s, gt_s, dgt_s, dqt_s, dgp_s, gated_s, dk_s, dv_s,
     bias_s, dacc_s, dw_s, dwo_s, grads_s, dpair_s,
-    part, r1, s1, r2, s2, r3, dense, r4, dwb, r5, s6, w6,
+    part, r1, s1, r2, dense, r4, dwb, r5, s6, w6,
     send_sem, recv_sem,
 ):
     r, c = lax.axis_index("row"), lax.axis_index("col")
     y, zh, core = c // 4, lax.rem(c // 2, 2), lax.rem(c, 2)
     sems = Sems(send_sem, recv_sem)
     barrier = pltpu.get_barrier_semaphore()
-    peers = [(row_peer(r, off), c) for off in ROW_OFFS] + [(r, col_peer(c, o)) for o in COL_OFFS]
+    me, level = zh * 8 + r, y * 2 + core
+    plane = []
+    for dz, dx, dh in PLANE_OFFS:
+        p = row_peer(r, (dz, dx))
+        plane.append((lax.rem(zh + dh, 2) * 8 + p, p, col_peer(c, (0, dh, 0))))
+    pillar = [col_peer(c, off) for off in PILLAR_OFFS]
+    peers = [(p, q) for _, p, q in plane] + [(r, q) for q in pillar]
     for peer in peers:
         pl.semaphore_signal(barrier, inc=1, device_id=peer, device_id_type=pl.DeviceIdType.MESH)
 
@@ -211,19 +224,24 @@
                 j = n * 4 + u
                 dst[j] = flat_s[pl.ds(j, TILE_ROWS, stride=TILE_COLS), :].astype(BF)
 
-    got[r] = turned[...]
+    got[me] = turned[...]
     pl.semaphore_wait(barrier, len(peers))
 
-    first = [sems.remote(turned, got.at[r], row_peer(r, off), c) for off in ROW_OFFS]
+    first = [sems.remote(turned, got.at[me], p, q) for _, p, q in plane]
     rows = pl.ds(pl.multiple_of(r * TILE_ROWS, TILE_ROWS), TILE_ROWS)
-    big = []
+    big = [[] for _ in range(COL_WIDTH)]
+
+    def spread(w, offs):
+        for off in offs:
+            p = row_peer(r, off)
+            big[w].append(sems.remote(actt.at[p * COL_WIDTH + w], act_s.at[w, rows, :], p, c))
+            big[w].append(sems.remote(gradt.at[p * COL_WIDTH + w], grad_s.at[w, rows, :], p, c))
+
+    near = [off for off in ROW_OFFS if off[0] == 0]
+    far = [off for off in ROW_OFFS if off[0] == 1]
     for w in range(COL_WIDTH):
-        now = []
-        for off in ROW_OFFS:
-            p = row_peer(r, off)
-            now.append(sems.remote(actt.at[p * COL_WIDTH + w], act_s.at[w, rows, :], p, c))
-            now.append(sems.remote(gradt.at[p * COL_WIDTH + w], grad_s.at[w, rows, :], p, c))
-        big.append(now)
+        spread(w, far)
+        spread(w, near)
     for w in range(COL_WIDTH):
         act_s[w, rows, :] = actt[r * COL_WIDTH + w]
         grad_s[w, rows, :] = gradt[r * COL_WIDTH + w]
@@ -231,28 +249,34 @@
         wt_s[n * PROJ : (n + 1) * PROJ, :] = ref[...].astype(F32).T.astype(BF)
     dw_s[...] = jnp.zeros_like(dw_s)
     dwo_s[...] = jnp.zeros_like(dwo_s)
+    dacc_s[...] = jnp.zeros_like(dacc_s)
 
     for cp in first:
         cp.wait_recv()
-    for s in range(SLOTS):
-        k = kb_ref[y, s]
-        tile = jnp.concatenate([got[2 * k], got[2 * k + 1]], axis=0).astype(F32)
-        tile = jnp.where(s < len_ref[y], tile, DEAD).T.astype(BF)
-        mine[:, :, s * BLOCK : (s + 1) * BLOCK] = tile.reshape(HEADS, TILE_COLS, BLOCK)
+    for z in range(2):
+        for s in range(SLOTS):
+            k = z * 8 + 2 * kb_ref[y, s]
+            tile = jnp.concatenate([got[k], got[k + 1]], axis=0).astype(F32)
+            tile = jnp.where(s < len_ref[y], tile, DEAD).T.astype(BF)
+            mine[z, :, :, s * BLOCK : (s + 1) * BLOCK] = tile.reshape(HEADS, TILE_COLS, BLOCK)
 
     def piece(ref, cc):
         at = pl.multiple_of(lax.rem(cc, 4) * TILE_COLS, TILE_COLS)
         return ref.at[cc // 4, :, pl.ds(at, TILE_COLS), :]
 
-    zc, sib = col_peer(c, (0, 1, 0)), col_peer(c, (0, 0, 1))
+    sib = col_peer(c, (0, 0, 1))
     ys = [col_peer(c, (n + 1, 0, 0)) for n in range(3)]
-    cz = sems.remote(mine, piece(full, c), r, zc)
-    to_y = [sems.remote(mine, piece(full, c), r, ys[n]) for n in range(3)]
-    cs = sems.remote(mine, piece(full, c), r, sib)
-    piece(full, c)[...] = mine[...]
-    cz.wait_recv()
-    to_y += [sems.remote(piece(full, zc), piece(full, zc), r, ys[n]) for n in range(3)]
-    fwd = [sems.remote(piece(full, zc), piece(full, zc), r, sib)]
+
+    def layer(cc, z):
+        return cc // 4 * 4 + z * 2 + core
+
+    cs = [sems.remote(mine.at[z], piece(full, layer(c, z)), r, sib) for z in range(2)]
+    to_y = [None] * 3
+    for n in (0, 2, 1):
+        to_y[n] = [sems.remote(mine.at[z], piece(full, layer(c, z)), r, ys[n]) for z in range(2)]
+    for z in range(2):
+        piece(full, layer(c, z))[...] = mine[z]
+    fwd = [None] * 3
 
     def column(w):
         for cp in big[w]:
@@ -260,24 +284,81 @@
         project(act_s, grad_s, wk_ref, wv_ref, wo_ref, wt_s, q4_s, qt_s, kt_s, vt_s, k_s, v_s,
                 gt_s, dgt_s, w)
 
-    def pass_on(z):
-        for n in range(3):
-            to_y[3 * z + n].wait_recv()
-            cc = col_peer(c, (3 - n, z, 0))
-            fwd.append(sems.remote(piece(full, cc), piece(full, cc), r, sib))
+    def pass_on(n):
+        fwd[n] = []
+        for z in range(2):
+            to_y[n][z].wait_recv()
+            cc = layer(col_peer(c, (3 - n, 0, 0)), z)
+            fwd[n].append(sems.remote(piece(full, cc), piece(full, cc), r, sib))
+
+    def block_of(t):
+        b = lax.rem(y + t, QBLOCKS)
+        return b, [kb_ref[b, s] for s in range(SLOTS)]
+
+    def pairs(t, lo, hi, between=None):
+        b, kbs = block_of(t)
+
+        @pl.loop(lo, hi)
+        def _(w):
+            one_pair(kbs, bias_s, q4_s, qt_s, kt_s, vt_s, k_s, v_s, gt_s, dgt_s, dqt_s, dgp_s,
+                     gated_s, dk_s, dv_s, dacc_s, w, b)
+            if between is not None:
+                pl.when(w == lo)(between)
+
+    def bias_block(t):
+        b, _ = block_of(t)
+        for h in range(HEADS):
+            bias_s[b, :, h * BLOCK : (h + 1) * BLOCK] = full[b, h].astype(F32).T
 
     column(0)
+    column(1)
+    for cp in cs:
+        cp.wait_recv()
+    bias_block(0)
+    pairs(0, 0, 2)
     pass_on(0)
-    column(1)
+    column(2)
+    pass_on(2)
+    for cp in fwd[0]:
+        cp.wait_recv()
+    bias_block(3)
+    pairs(3, 0, 2)
     pass_on(1)
-    column(2)
     column(3)
-    cs.wait_recv()
-    for cp in fwd:
-        cp.wait_recv()
+    for t, n in ((1, 2), (2, 1)):
+        for cp in fwd[n]:
+            cp.wait_recv()
+        bias_block(t)
+        pairs(t, 0, 2)
+
+    def gather_grads(lo, hi):
+        @pl.loop(lo, hi)
+        def _(w):
+            collect(kb_ref, len_ref, act_s, grad_s, dqt_s, dgp_s, gated_s, dk_s, dv_s, dw_s, dwo_s,
+                    grads_s, w)
+
+    cd = []
+    w_all = jnp.concatenate([ref[...] for ref in (wq_ref, wk_ref, wv_ref, wg_ref)], axis=1)
+
+    def d_pair(w):
+        back = mm(w_all, grads_s[w])
+        for b in range(QBLOCKS):
+            at = slice(b * BLOCK, (b + 1) * BLOCK)
+            dpair_s[w, at, :] = back[:, at].T.astype(BF)
+
+    def give(w, offs):
+        for off in offs:
+            p = row_peer(r, off)
+            src = dpair_s.at[w, pl.ds(pl.multiple_of(p * TILE_ROWS, TILE_ROWS), TILE_ROWS), :]
+            cd.append(sems.remote(src, dp_ref.at[r * COL_WIDTH + w], p, c))
+
+    gather_grads(0, 2)
+    for w in range(2):
+        d_pair(w)
+        give(w, far)
+        give(w, near)
 
     c1, c2 = [], []
-    total = None
 
     def merge(t):
         for n in range(2):
@@ -287,112 +368,92 @@
             s1[t, n] = (own.astype(F32) + r1[t, n].astype(F32)).astype(BF)
 
     for t in range(QBLOCKS):
-        b = lax.rem(y + 1 + t, QBLOCKS)
-        kbs = [kb_ref[b, s] for s in range(SLOTS)]
+        b, _ = block_of(1 + t)
+        if t > 0:
+            c2.append(sems.later(s1.at[t - 1], r2.at[t - 1], r, ys[t - 1]))
+
+        def between():
+            merge(t - 1)
+            c2[t - 1].start()
+
+        pairs(1 + t, 2, COL_WIDTH, between if t > 0 else None)
         for h in range(HEADS):
-            bias_s[0, :, h * BLOCK : (h + 1) * BLOCK] = full[b, h].astype(F32).T
-        dacc_s[...] = jnp.zeros_like(dacc_s)
-
-        @pl.loop(0, COL_WIDTH)
-        def _(w):
-            one_pair(kbs, bias_s, q4_s, qt_s, kt_s, vt_s, k_s, v_s, gt_s, dgt_s, dqt_s, dgp_s,
-                     gated_s, dk_s, dv_s, dacc_s, w, b)
-
-        for h in range(HEADS):
-            part[t, h] = dacc_s[:, h * BLOCK : (h + 1) * BLOCK].T.astype(BF)
+            part[t, h] = dacc_s[b, :, h * BLOCK : (h + 1) * BLOCK].T.astype(BF)
         now = []
         for n in range(2):
             at = pl.multiple_of((2 * n + 1 - core) * TILE_COLS, TILE_COLS)
             now.append(sems.remote(part.at[t, :, pl.ds(at, TILE_COLS), :], r1.at[t, n], r, sib))
         c1.append(now)
-        if t > 0:
-            merge(t - 1)
-            c2.append(sems.remote(s1.at[t - 1], r2.at[t - 1], r, ys[t - 1]))
-
-    @pl.loop(0, COL_WIDTH)
-    def _(w):
-        collect(kb_ref, len_ref, act_s, grad_s, dqt_s, dgp_s, gated_s, dk_s, dv_s, dw_s, dwo_s,
-                grads_s, w)
-
+
+    gather_grads(2, COL_WIDTH)
     for n in range(4):
         at = slice(n * PROJ, (n + 1) * PROJ)
         dwb[at, :] = dw_s[at, :].T.astype(BF)
-    dwb[4 * PROJ :, :] = dwo_s[...].astype(BF)
+    dwb[4 * PROJ : WROWS, :] = dwo_s[...].astype(BF)
+    dwb[WROWS:, :] = jnp.zeros((WPAD - WROWS, PROJ), BF)
     c5 = []
-    for n, off in enumerate(ROW_OFFS):
-        p = row_peer(r, off)
-        src = dwb.at[pl.ds(pl.multiple_of(p * WPART, 16), WPART), :]
-        c5.append(sems.remote(src, r5.at[n], p, c))
+    for g, p, q in plane:
+        src = dwb.at[pl.ds(pl.multiple_of(g * WPART, 16), WPART), :]
+        c5.append(sems.remote(src, r5.at[me], p, q))
+    myrows = pl.ds(pl.multiple_of(me * WPART, 16), WPART)
+    r5[me] = dwb[myrows, :]
+    for w in range(2, COL_WIDTH):
+        d_pair(w)
+        give(w, near)
     merge(3)
     for cp in c2:
         cp.wait_recv()
 
-    def share(z):
+    for z in range(2):
         acc = s1[3, z].astype(F32)
         for m in range(3):
             acc = acc + r2[m, z].astype(F32)
-        return acc
-
-    s2[...] = share(1 - zh).astype(BF)
-    c3 = sems.remote(s2, r3, r, zc)
-    cd = []
-    w_all = jnp.concatenate([ref[...] for ref in (wq_ref, wk_ref, wv_ref, wg_ref)], axis=1)
-    for w in range(COL_WIDTH):
-        back = mm(w_all, grads_s[w])
-        for b in range(QBLOCKS):
-            at = slice(b * BLOCK, (b + 1) * BLOCK)
-            dpair_s[w, at, :] = back[:, at].T.astype(BF)
-        for off in ROW_OFFS:
-            p = row_peer(r, off)
-            src = dpair_s.at[w, pl.ds(pl.multiple_of(p * TILE_ROWS, TILE_ROWS), TILE_ROWS), :]
-            cd.append(sems.remote(src, dp_ref.at[r * COL_WIDTH + w], p, c))
-        if w == 1:
-            for cp in c5:
-                cp.wait_recv()
-            tot = dwb[pl.ds(pl.multiple_of(r * WPART, 16), WPART), :].astype(F32)
-            for n in range(7):
-                tot = tot + r5[n].astype(F32)
-            s6[...] = tot.astype(BF)
-            w6[c] = s6[...]
-            c6 = [sems.remote(s6, w6.at[c], r, col_peer(c, off)) for off in COL_OFFS]
+        tiles = [
+            acc[:, :, s * BLOCK : (s + 1) * BLOCK].reshape(PROJ, BLOCK).T for s in range(SLOTS)
+        ]
+        for k in range(QBLOCKS):
+            val = jnp.zeros((BLOCK, PROJ), F32)
+            for s in range(SLOTS):
+                hit = (kb_ref[y, s] == k) & (s < len_ref[y])
+                val = val + jnp.where(hit, tiles[s], 0.0)
+            dense[z * QBLOCKS + k] = val.astype(BF)
+
+    def share(g):
+        at = pl.multiple_of(lax.rem(g, 2) * TILE_ROWS, TILE_ROWS)
+        return dense.at[g // 2, pl.ds(at, TILE_ROWS), :]
+
+    c4 = [sems.remote(share(g), r4.at[me], p, q) for g, p, q in plane]
+    r4[me] = share(me)[...]
+    for cp in c5:
+        cp.wait_recv()
+    tot = r5[0].astype(F32)
+    for n in range(1, PLANE):
+        tot = tot + r5[n].astype(F32)
+    s6[...] = tot.astype(BF)
+    w6[level] = s6[...]
+    c6 = [sems.remote(s6, w6.at[level], r, q) for q in pillar]
+    for w in range(2, COL_WIDTH):
+        give(w, far)
     for w in range(COL_WIDTH):
         dp_ref[r * COL_WIDTH + w] = dpair_s[w, rows, :]
-    acc = share(zh)
-    c3.wait_recv()
-    acc = acc + r3[...].astype(F32)
-    tiles = [
-        acc[:, :, s * BLOCK : (s + 1) * BLOCK].reshape(PROJ, BLOCK).T for s in range(SLOTS)
+    for cp in c6:
+        cp.wait_recv()
+    tot = w6[0].astype(F32)
+    for n in range(1, PILLAR):
+        tot = tot + w6[n].astype(F32)
+    wsum_ref[myrows, :] = tot.astype(BF)
+    c7 = [
+        sems.remote(wsum_ref.at[myrows, :], wsum_ref.at[myrows, :], p, q) for _, p, q in plane
     ]
-    for k in range(QBLOCKS):
-        val = jnp.zeros((BLOCK, PROJ), F32)
-        for s in range(SLOTS):
-            hit = (kb_ref[y, s] == k) & (s < len_ref[y])
-            val = val + jnp.where(hit, tiles[s], 0.0)
-        dense[k * BLOCK : (k + 1) * BLOCK, :] = val.astype(BF)
-    c4 = []
-    for n, off in enumerate(ROW_OFFS):
-        p = row_peer(r, off)
-        src = dense.at[pl.ds(pl.multiple_of(p * TILE_ROWS, TILE_ROWS), TILE_ROWS), :]
-        c4.append(sems.remote(src, r4.at[n], p, c))
-    for cp in c6:
-        cp.wait_recv()
-    tot = w6[0].astype(F32)
-    for n in range(1, COLS):
-        tot = tot + w6[n].astype(F32)
-    myrows = pl.ds(pl.multiple_of(r * WPART, 16), WPART)
-    wsum_ref[myrows, :] = tot
-    c7 = [
-        sems.remote(wsum_ref.at[myrows, :], wsum_ref.at[myrows, :], row_peer(r, off), c)
-        for off in ROW_OFFS
-    ]
-    val = dense[rows, :].astype(F32)
-    for n in range(7):
-        c4[n].wait_recv()
+    for cp in c4:
+        cp.wait_recv()
+    val = r4[0].astype(F32)
+    for n in range(1, PLANE):
         val = val + r4[n].astype(F32)
     db_ref[...] = val.T
     for cp in cd + c7:
         cp.wait_recv()
-    for cp in sum(big, []) + first + [cz, cs, c3] + to_y + fwd + sum(c1, []) + c2 + c4 + c5 + c6 + c7 + cd:
+    for cp in sum(big + to_y + fwd + c1, []) + first + cs + c2 + c4 + c5 + c6 + c7 + cd:
         cp.wait_send()
 
 
@@ -412,7 +473,7 @@
         out_shape=(
             jax.ShapeDtypeStruct(flip, BF),
             jax.ShapeDtypeStruct((PROJ, TILE_ROWS), F32),
-            jax.ShapeDtypeStruct((WROWS, PROJ), F32),
+            jax.ShapeDtypeStruct((WPAD, PROJ), BF),
         ),
         in_specs=[smem] * 2 + [vmem] * 8,
         out_specs=(vmem, vmem, vmem),
@@ -420,8 +481,8 @@
             pltpu.VMEM((TILE_ROWS * TILE_COLS, PROJ), F32),
             pltpu.VMEM(flip, BF), pltpu.VMEM(flip, BF),
             pltpu.VMEM(cols, BF), pltpu.VMEM(cols, BF),
-            pltpu.VMEM((TILE_ROWS, PROJ), BF), pltpu.VMEM((ROWS, TILE_ROWS, PROJ), BF),
-            pltpu.VMEM(piece, BF), pltpu.VMEM(whole, BF),
+            pltpu.VMEM((TILE_ROWS, PROJ), BF), pltpu.VMEM((PLANE, TILE_ROWS, PROJ), BF),
+            pltpu.VMEM((2, *piece), BF), pltpu.VMEM(whole, BF),
             pltpu.VMEM((4 * PROJ, PROJ), BF),
             pltpu.VMEM((COL_WIDTH, QBLOCKS, PROJ, HEADS * BLOCK), BF),
             pltpu.VMEM(tiles, BF), pltpu.VMEM(tiles, BF), pltpu.VMEM(tiles, BF),
@@ -429,16 +490,15 @@
             pltpu.VMEM(tiles, F32), pltpu.VMEM(tiles, F32),
             pltpu.VMEM(tiles, BF), pltpu.VMEM(tiles, BF), pltpu.VMEM(tiles, BF),
             pltpu.VMEM(slots, F32), pltpu.VMEM(slots, F32),
-            pltpu.VMEM((1, WIDE, HEADS * BLOCK), F32),
-            pltpu.VMEM((WIDE, HEADS * BLOCK), F32),
+            pltpu.VMEM((QBLOCKS, WIDE, HEADS * BLOCK), F32),
+            pltpu.VMEM((QBLOCKS, WIDE, HEADS * BLOCK), F32),
             pltpu.VMEM((4 * PROJ, PROJ), F32), pltpu.VMEM((PROJ, PROJ), F32),
             pltpu.VMEM((COL_WIDTH, 4 * PROJ, TOKENS), BF), pltpu.VMEM(cols, BF),
             pltpu.VMEM(whole, BF), pltpu.VMEM((QBLOCKS, 2, *piece), BF),
             pltpu.VMEM((QBLOCKS, 2, *piece), BF), pltpu.VMEM((3, 2, *piece), BF),
-            pltpu.VMEM(piece, BF), pltpu.VMEM(piece, BF),
-            pltpu.VMEM((TOKENS, PROJ), BF), pltpu.VMEM((7, TILE_ROWS, PROJ), BF),
-            pltpu.VMEM((WROWS, PROJ), BF), pltpu.VMEM((7, WPART, PROJ), BF),
-            pltpu.VMEM((WPART, PROJ), BF), pltpu.VMEM((COLS, WPART, PROJ), BF),
+            pltpu.VMEM((2 * QBLOCKS, BLOCK, PROJ), BF), pltpu.VMEM((PLANE, TILE_ROWS, PROJ), BF),
+            pltpu.VMEM((WPAD, PROJ), BF), pltpu.VMEM((PLANE, WPART, PROJ), BF),
+            pltpu.VMEM((WPART, PROJ), BF), pltpu.VMEM((PILLAR, WPART, PROJ), BF),
             dma((N_SEMS,)), dma((N_SEMS,)),
         ],
         compiler_params=pltpu.CompilerParams(
@@ -457,7 +517,9 @@
     )
     d_pair = jnp.transpose(dp, (1, 0, 2))
     d_bias = jnp.transpose(db.reshape(HEADS, TILE_COLS, TILE_ROWS), (0, 2, 1))
-    return (d_pair, d_bias) + tuple(ws[n * PROJ : (n + 1) * PROJ] for n in range(5))
+    return (d_pair, d_bias) + tuple(
+        ws[n * PROJ : (n + 1) * PROJ].astype(F32) for n in range(5)
+    )
 
 
 def solution(mesh):

time: 90.7 us -> 74.8 us (0.82)
  Pallas kernels: 86.1 us -> 70.2 us
    pallas_call x1, Pallas kernels: 86.1 us -> 70.2 us  [fused(): pl.pallas_call(fused_kernel, out_shape=(jax.ShapeDtypeStruct(flip, BF), j...]
where the time goes in v4:
time: 74.8 us; the launch traced here: 74.6 us
  Pallas kernels  70.2 us (94%)
  local copies, waits for them, and re-layouts  2.99 us (4%)
    pallas_call x1, Pallas kernels, fused(): pl.pallas_call(fused_kernel, out_shape=(jax.ShapeDtypeStruct(flip, BF), j...  70.2 us
    unnamed x6, local copies, waits for them, and re-layouts  2.99 us

profile of v4, /device:TPU:1, one launch (start us, length us, event | category | flops | bytes accessed | tf_op | source)
XLA Modules:
  0.0 74.6 jit_solution(16100816814839164221)
XLA Ops:
  0.6 70.2 %attend_back.1 = (bf16[32,64,128]{2,1,0:T(8,128)(2,1)}, f32[128,64]{1,0:T(8,128)}, bf16[768,128]{1,0:T(8,128)(2,1)}) custom-call(s32[4,3]{1,0:T(4,128)} %kb_ref.1, s32[4]{0:T(128)} %len_ref.1, bf16[64,32,128]{2,1,0:T(8,128)(2,1)} %pair_ref.1, bf16[64,32,128]{2,1,0:T(8,128)(2,1)} %cot_ref.1, bf16[128,64]{1,0:T(8,128)(2,1)} %bitcast.9, ...), custom_call_target="tpu_custom_call" | custom-call | tf_op jit(solution)/shard_map/attend_back/pallas_call | solution.py:471
  70.8 0.0 copy-start
  70.8 2.2 %copy.17 = bf16[64,32,128]{2,1,0:T(8,128)(2,1)} copy(bf16[64,32,128]{2,0,1:T(8,128)(2,1)} %bitcast.7) | data formatting | bytes 1048576
  73.1 0.0 copy-done
  73.1 0.0 copy-start.1
  73.1 0.7 slice_convert_fusion
  73.8 0.1 copy-done.1
  73.9 0.6 copy.19
Async XLA Ops:
  70.8 2.2 %copy-start = (bf16[768,128]{1,0:T(8,128)(2,1)S(1)}, bf16[768,128]{1,0:T(8,128)(2,1)}, u32[]{:S(2)}) copy-start(bf16[768,128]{1,0:T(8,128)(2,1)} %get-tuple-element.12) | copy-start | bytes 589828
  73.1 0.9 %copy-start.1 = (f32[128,64]{1,0:T(8,128)S(1)}, f32[128,64]{1,0:T(8,128)}, u32[]{:S(2)}) copy-start(f32[128,64]{1,0:T(8,128)} %get-tuple-element.11) | copy-start | bytes 98308

commit v5 on v4

v5 whole, which is shorter than its diff:
```python
import functools

import jax
import jax.numpy as jnp
from jax import lax
from jax.experimental import pallas as pl
from jax.experimental.pallas import tpu as pltpu
from jax.sharding import PartitionSpec as P

BF = jnp.bfloat16
F32 = jnp.float32
HEADS = 4
HEAD_DIM = 32
PROJ = HEADS * HEAD_DIM
BLOCK = 128
QBLOCKS = 4
SLOTS = 3
TOKENS = QBLOCKS * BLOCK
WIDE = SLOTS * BLOCK
ROWS = 8
COLS = 16
TILE_ROWS = TOKENS // ROWS
TILE_COLS = TOKENS // COLS
COL_WIDTH = TILE_COLS // ROWS
WROWS = 5 * PROJ
PLANE = 16
PILLAR = 8
WPART = 48
WPAD = WPART * PLANE
DEAD = -1e30
SCALE = HEAD_DIM ** -0.5

ROW_OFFS = [(dz, dx) for dz in range(2) for dx in range(4)][1:]
PLANE_OFFS = [(dz, dx, dh) for dh in range(2) for dz in range(2) for dx in range(4)][1:]
FLAT_OFFS = [(dx, dy) for dx in range(4) for dy in range(4)][1:]
PILLAR_OFFS = [(dz, dh, dc) for dz in range(2) for dh in range(2) for dc in range(2)][1:]


def row_peer(r, off):
    z, x = r // 4, lax.rem(r, 4)
    return lax.rem(z + off[0], 2) * 4 + lax.rem(x + off[1], 4)


def col_peer(c, off):
    y, z, k = c // 4, lax.rem(c // 2, 2), lax.rem(c, 2)
    return lax.rem(y + off[0], 4) * 4 + lax.rem(z + off[1], 2) * 2 + lax.rem(k + off[2], 2)


def remote(src, dst, ssem, rsem, r, c):
    return pltpu.make_async_remote_copy(
        src_ref=src,
        dst_ref=dst,
        send_sem=ssem,
        recv_sem=rsem,
        device_id=(r, c),
        device_id_type=pl.DeviceIdType.MESH,
    )


NT = (((1,), (1,)), ((), ()))
NN = (((1,), (0,)), ((), ()))


def mm(a, b, dims=NN):
    return lax.dot_general(a, b, dims, preferred_element_type=F32)


def head_rows(x):
    head_of = lax.broadcasted_iota(jnp.int32, x.shape, 0) // HEAD_DIM
    return jnp.concatenate(
        [jnp.where(head_of == h, x, jnp.zeros_like(x)) for h in range(HEADS)], axis=1
    )


def head_cols(x):
    head_of = lax.broadcasted_iota(jnp.int32, x.shape, 1) // HEAD_DIM
    return jnp.concatenate(
        [jnp.where(head_of == h, x, jnp.zeros_like(x)) for h in range(HEADS)], axis=0
    )


def project(act_ref, grad_ref, wq_ref, wk_ref, wv_ref, wo_ref, wt_s, q4_s, qn_s, kt_s, vt_s, k_s, v_s,
            gt_s, dgt_s, xt_s, w):
    x = act_ref[w]
    turned = mm(wt_s[...], x, NT)
    qt = (turned[:PROJ] * SCALE).astype(BF)
    kt = turned[PROJ : 2 * PROJ].astype(BF)
    vt = turned[2 * PROJ : 3 * PROJ].astype(BF)
    for b in range(QBLOCKS):
        cols = slice(b * BLOCK, (b + 1) * BLOCK)
        q4_s[w, b] = head_rows(qt[:, cols])
        kt_s[w, b] = kt[:, cols]
        vt_s[w, b] = vt[:, cols]
        gt_s[w, b] = jax.nn.sigmoid(turned[3 * PROJ :, cols])
    dgt = mm(wo_ref[...], grad_ref[w], NT)
    qkv = mm(x, jnp.concatenate([wq_ref[...], wk_ref[...], wv_ref[...]], axis=1))
    q = (qkv[:, :PROJ] * SCALE).astype(BF)
    k = qkv[:, PROJ : 2 * PROJ].astype(BF)
    v = qkv[:, 2 * PROJ :].astype(BF)
    for b in range(QBLOCKS):
        rows = slice(b * BLOCK, (b + 1) * BLOCK)
        dgt_s[w, b] = dgt[:, rows]
        k_s[w, b] = k[rows]
        qn_s[w, b] = head_cols(q[rows])
        xt_s[w, :, rows] = x[rows].astype(F32).T.astype(BF)
        v_s[w, b] = v[rows]


def one_pair(kbs, bias_s, q4_s, qn_s, kt_s, vt_s, k_s, v_s, gt_s, dgt_s, dqt_s, dgp_s, gated_s,
             dk_s, dv_s, dacc_s, w, b):
    def chosen(ref, axis):
        return jnp.concatenate([ref[w, kb] for kb in kbs], axis=axis)

    heads = [slice(h * BLOCK, (h + 1) * BLOCK) for h in range(HEADS)]
    scores = mm(chosen(k_s, 0), q4_s[w, b]) + bias_s[b]
    e = jnp.exp(scores - jnp.max(scores, axis=0, keepdims=True))
    e_low = e.astype(BF)
    vt = chosen(vt_s, 1)
    ones = jnp.ones((16, WIDE), BF)
    atts, invs = [], []
    for h in range(HEADS):
        lhs = jnp.concatenate([vt[h * HEAD_DIM : (h + 1) * HEAD_DIM], ones], axis=0)
        both = mm(lhs, e_low[:, heads[h]])
        part = 1.0 / both[HEAD_DIM : HEAD_DIM + 1]
        atts.append(both[:HEAD_DIM] * part)
        invs.append(jnp.broadcast_to(part, (HEAD_DIM, BLOCK)))
    att = jnp.concatenate(atts, axis=0)
    inv = jnp.concatenate(invs, axis=0)
    g = gt_s[w, b]
    datt = dgt_s[w, b] * g
    gated_s[w, b] = (g * att).astype(BF)
    dgp_s[w, b] = (datt * att * (1.0 - g)).astype(BF)
    dn = (datt * inv).astype(BF)
    prod = dn.astype(F32) * att
    delta = jnp.concatenate(
        [
            jnp.sum(prod[h * HEAD_DIM : (h + 1) * HEAD_DIM], axis=0, keepdims=True)
            for h in range(HEADS)
        ],
        axis=1,
    )
    ds = e * (mm(chosen(v_s, 0), head_rows(dn)) - delta)
    dacc_s[b] += ds
    ds_low = ds.astype(BF)
    kt = chosen(kt_s, 1)
    for h in range(HEADS):
        hs = slice(h * HEAD_DIM, (h + 1) * HEAD_DIM)
        dqt_s[w, b, hs, :] = (mm(kt[hs], ds_low[:, heads[h]]) * SCALE).astype(BF)
    dk = mm(ds_low, qn_s[w, b])
    dv = mm(e_low, head_cols(dn.astype(F32).T.astype(BF)))
    for s in range(SLOTS):
        dk_s[w, b, s] = dk[s * BLOCK : (s + 1) * BLOCK]
        dv_s[w, b, s] = dv[s * BLOCK : (s + 1) * BLOCK]


def collect(kb_ref, len_ref, act_ref, grad_ref, xt_s, dqt_s, dgp_s, gated_s, dk_s, dv_s, dw_s,
            dwkv_s, dwo_s, ga_s, gb_s, w):
    for k in range(QBLOCKS):
        dk = jnp.zeros((BLOCK, PROJ), F32)
        dv = jnp.zeros((BLOCK, PROJ), F32)
        for b in range(QBLOCKS):
            slot = jnp.int32(SLOTS)
            for s in range(SLOTS):
                slot = jnp.where((kb_ref[b, s] == k) & (s < len_ref[b]), s, slot)
            listed = slot < SLOTS
            at = jnp.minimum(slot, SLOTS - 1)
            dk = dk + jnp.where(listed, dk_s[w, b, at], 0.0)
            dv = dv + jnp.where(listed, dv_s[w, b, at], 0.0)
        cols = slice(k * BLOCK, (k + 1) * BLOCK)
        gb_s[w, cols, :PROJ] = dk.astype(BF)
        gb_s[w, cols, PROJ:] = dv.astype(BF)
        ga_s[w, :PROJ, cols] = dqt_s[w, k]
        ga_s[w, PROJ:, cols] = dgp_s[w, k]
    dw_s[...] += mm(ga_s[w], act_ref[w])
    dwkv_s[...] += mm(xt_s[w], gb_s[w])
    gated = jnp.concatenate([gated_s[w, b] for b in range(QBLOCKS)], axis=1)
    dwo_s[...] += mm(gated, grad_ref[w])


(S_BIAS, S_ACT, S_GRAD, S_OWN, S_Y, S_FWD, S_SIB, S_SUM, S_TILE, S_PAIR, S_PART, S_LEVEL, S_LAST) = range(13)
(R_BIAS, R_ACT, R_GRAD, R_OWN, R_Y, R_FWD, R_SIB, R_SUM, R_TILE, R_PAIR, R_PART, R_LEVEL, R_LAST) = (
    0, 1, 5, 9, 10, 13, 16, 20, 23, 24, 28, 29, 30,
)
N_SEND, N_RECV = 13, 31


def settle(ref, sem):
    pltpu.make_async_copy(ref, ref, sem).wait()


def fused_kernel(
    kb_ref, len_ref, pair_ref, cot_ref, bias_ref, wq_ref, wk_ref, wv_ref, wg_ref, wo_ref,
    dp_ref, db_ref, wsum_ref,
    flat_s, actt, gradt, act_s, grad_s, turned, got, mine, full,
    wt_s, q4_s, qn_s, kt_s, vt_s, k_s, v_s, gt_s, dgt_s, dqt_s, dgp_s, gated_s, dk_s, dv_s,
    bias_s, dacc_s, dw_s, dwkv_s, dwo_s, xt_s, ga_s, gb_s, dpair_s, raw, back_s, wtot, local_sem,
    part, r1, s1, r2, dense, r4, dwb, r5, s6, w6,
    send_sem, recv_sem,
):
    r, c = lax.axis_index("row"), lax.axis_index("col")
    y, zh, core = c // 4, lax.rem(c // 2, 2), lax.rem(c, 2)

    def later(src, dst, si, ri, p, q):
        return remote(src, dst, send_sem.at[si], recv_sem.at[ri], p, q)

    def send(*what):
        later(*what).start()

    def arrived(ref, ri):
        settle(ref, recv_sem.at[ri])

    barrier = pltpu.get_barrier_semaphore()
    me, spot, level = zh * 8 + r, y * 4 + lax.rem(r, 4), r // 4 * 4 + zh * 2 + core
    plane = []
    for dz, dx, dh in PLANE_OFFS:
        p = row_peer(r, (dz, dx))
        plane.append((lax.rem(zh + dh, 2) * 8 + p, p, col_peer(c, (0, dh, 0))))
    flat = []
    for dx, dy in FLAT_OFFS:
        p, q = row_peer(r, (0, dx)), col_peer(c, (dy, 0, 0))
        flat.append((q // 4 * 4 + lax.rem(p, 4), p, q))
    pillar = [(row_peer(r, (dz, 0)), col_peer(c, (0, dh, dc))) for dz, dh, dc in PILLAR_OFFS]
    peers = [(p, q) for _, p, q in plane]
    peers += [(p, q) for (_, p, q), off in zip(flat, FLAT_OFFS) if off[1]]
    peers += [peer for peer, off in zip(pillar, PILLAR_OFFS) if off[2]]
    for peer in peers:
        pl.semaphore_signal(barrier, inc=1, device_id=peer, device_id_type=pl.DeviceIdType.MESH)

    loads = [
        pltpu.make_async_copy(src, raw.at[n], local_sem.at[n])
        for n, src in enumerate((pair_ref, cot_ref))
    ]
    for cp in loads:
        cp.start()
    turned[...] = bias_ref[...].astype(F32).T.astype(BF)
    for n, dst in enumerate((actt, gradt)):
        loads[n].wait()
        flat_s[...] = raw[n].astype(F32).reshape(TILE_ROWS * TILE_COLS, PROJ)

        @pl.loop(0, TILE_COLS // 4)
        def _(m):
            for u in range(4):
                j = m * 4 + u
                dst[j] = flat_s[pl.ds(j, TILE_ROWS, stride=TILE_COLS), :].astype(BF)

    got[me] = turned[...]
    pl.semaphore_wait(barrier, len(peers))

    for _, p, q in plane:
        send(turned, got.at[me], S_BIAS, R_BIAS, p, q)
    rows = pl.ds(pl.multiple_of(r * TILE_ROWS, TILE_ROWS), TILE_ROWS)
    def spread(w, offs):
        for off in offs:
            p = row_peer(r, off)
            j = p * COL_WIDTH + w
            send(actt.at[j], act_s.at[w, rows, :], S_ACT, R_ACT + w, p, c)
            send(gradt.at[j], grad_s.at[w, rows, :], S_GRAD, R_GRAD + w, p, c)

    near = [off for off in ROW_OFFS if off[0] == 0]
    far = [off for off in ROW_OFFS if off[0] == 1]
    for w in range(COL_WIDTH):
        spread(w, far)
        spread(w, near)
    for w in range(COL_WIDTH):
        act_s[w, rows, :] = actt[r * COL_WIDTH + w]
        grad_s[w, rows, :] = gradt[r * COL_WIDTH + w]
    for n, ref in enumerate((wq_ref, wk_ref, wv_ref, wg_ref)):
        wt_s[n * PROJ : (n + 1) * PROJ, :] = ref[...].astype(F32).T.astype(BF)
    dw_s[...] = jnp.zeros_like(dw_s)
    dwkv_s[...] = jnp.zeros_like(dwkv_s)
    dwo_s[...] = jnp.zeros_like(dwo_s)
    dacc_s[...] = jnp.zeros_like(dacc_s)

    arrived(got.at[pl.ds(0, PLANE - 1)], R_BIAS)
    for z in range(2):
        for s in range(SLOTS):
            k = z * 8 + 2 * kb_ref[y, s]
            tile = jnp.concatenate([got[k], got[k + 1]], axis=0).astype(F32)
            tile = jnp.where(s < len_ref[y], tile, DEAD).T.astype(BF)
            mine[z, :, :, s * BLOCK : (s + 1) * BLOCK] = tile.reshape(HEADS, TILE_COLS, BLOCK)

    def piece(ref, cc):
        at = pl.multiple_of(lax.rem(cc, 4) * TILE_COLS, TILE_COLS)
        return ref.at[cc // 4, :, pl.ds(at, TILE_COLS), :]

    sib = col_peer(c, (0, 0, 1))
    ys = [col_peer(c, (n + 1, 0, 0)) for n in range(3)]

    def layer(cc, z):
        return cc // 4 * 4 + z * 2 + core

    for z in range(2):
        send(mine.at[z], piece(full, layer(c, z)), S_OWN, R_OWN, r, sib)
    for n in (1, 0, 2):
        for z in range(2):
            send(mine.at[z], piece(full, layer(c, z)), S_Y, R_Y + n, r, ys[n])
    for z in range(2):
        piece(full, layer(c, z))[...] = mine[z]
    def column(w):
        most = pl.ds(0, TOKENS - TILE_ROWS)
        arrived(act_s.at[w, most, :], R_ACT + w)
        arrived(grad_s.at[w, most, :], R_GRAD + w)
        project(act_s, grad_s, wq_ref, wk_ref, wv_ref, wo_ref, wt_s, q4_s, qn_s, kt_s, vt_s, k_s, v_s,
                gt_s, dgt_s, xt_s, w)

    def pass_on(n):
        arrived(mine, R_Y + n)
        for z in range(2):
            cc = layer(col_peer(c, (3 - n, 0, 0)), z)
            send(piece(full, cc), piece(full, cc), S_FWD, R_FWD + n, r, sib)

    def block_of(t):
        b = lax.rem(y + t, QBLOCKS)
        return b, [kb_ref[b, s] for s in range(SLOTS)]

    def pairs(t, lo, hi, between=None):
        b, kbs = block_of(t)

        @pl.loop(lo, hi)
        def _(w):
            one_pair(kbs, bias_s, q4_s, qn_s, kt_s, vt_s, k_s, v_s, gt_s, dgt_s, dqt_s, dgp_s,
                     gated_s, dk_s, dv_s, dacc_s, w, b)
            if between is not None:
                pl.when(w == lo + 1)(between)

    def bias_block(t):
        b, _ = block_of(t)
        for h in range(HEADS):
            bias_s[b, :, h * BLOCK : (h + 1) * BLOCK] = full[b, h].astype(F32).T

    def gather_grads(lo, hi):
        @pl.loop(lo, hi)
        def _(w):
            collect(kb_ref, len_ref, act_s, grad_s, xt_s, dqt_s, dgp_s, gated_s, dk_s, dv_s, dw_s,
                    dwkv_s, dwo_s, ga_s, gb_s, w)

    w_qg = jnp.concatenate([wq_ref[...], wg_ref[...]], axis=1)
    w_kv = jnp.concatenate([wk_ref[...], wv_ref[...]], axis=1)

    def d_pair(w):
        back = mm(w_qg, ga_s[w]) + mm(w_kv, gb_s[w], NT)
        for b in range(QBLOCKS):
            at = slice(b * BLOCK, (b + 1) * BLOCK)
            dpair_s[w, at, :] = back[:, at].T.astype(BF)

    def give(w, offs):
        for off in offs:
            p = row_peer(r, off)
            src = dpair_s.at[w, pl.ds(pl.multiple_of(p * TILE_ROWS, TILE_ROWS), TILE_ROWS), :]
            send(src, back_s.at[r * COL_WIDTH + w], S_PAIR, R_PAIR + w, p, c)

    c2 = [None] * QBLOCKS

    def merge(t):
        arrived(r1.at[t], R_SIB + t)
        for n in range(2):
            at = pl.multiple_of((2 * n + core) * TILE_COLS, TILE_COLS)
            own = part[t, :, pl.ds(at, TILE_COLS), :]
            s1[t, n] = (own.astype(F32) + r1[t, n].astype(F32)).astype(BF)

    def merge_and_send(t):
        merge(t)
        c2[t].start()

    def close_block(t):
        b, _ = block_of(t)
        for h in range(HEADS):
            part[t, h] = dacc_s[b, :, h * BLOCK : (h + 1) * BLOCK].T.astype(BF)
        for n in range(2):
            at = pl.multiple_of((2 * n + 1 - core) * TILE_COLS, TILE_COLS)
            send(part.at[t, :, pl.ds(at, TILE_COLS), :], r1.at[t, n], S_SIB, R_SIB + t, r, sib)
        if t > 0:
            c2[t] = later(s1.at[t], r2.at[t - 1], S_SUM, R_SUM + t - 1, r, ys[t - 1])

    column(0)
    arrived(mine, R_OWN)
    bias_block(0)
    pairs(0, 0, 1)
    column(1)
    pass_on(1)
    pairs(0, 1, 2)
    pass_on(0)
    last = None
    for t, n in ((2, 1), (3, 0), (1, 2)):
        arrived(mine, R_FWD + n)
        bias_block(t)
        if last is None:
            pairs(t, 0, 2)
            column(2)
            column(3)
            pass_on(2)
            pairs(t, 2, COL_WIDTH)
        else:
            pairs(t, 0, COL_WIDTH, functools.partial(merge_and_send, last))
        close_block(t)
        last = t

    gather_grads(0, 2)
    for w in range(2):
        d_pair(w)
        give(w, far)
        give(w, near)
    merge_and_send(last)
    pairs(0, 2, 3)
    gather_grads(2, 3)
    d_pair(2)
    give(2, far)
    give(2, near)
    pairs(0, 3, COL_WIDTH)
    close_block(0)
    gather_grads(3, COL_WIDTH)
    dwb[:PROJ, :] = dw_s[:PROJ, :].T.astype(BF)
    dwb[PROJ : 2 * PROJ, :] = dwkv_s[:, :PROJ].astype(BF)
    dwb[2 * PROJ : 3 * PROJ, :] = dwkv_s[:, PROJ:].astype(BF)
    dwb[3 * PROJ : 4 * PROJ, :] = dw_s[PROJ:, :].T.astype(BF)
    dwb[4 * PROJ : WROWS, :] = dwo_s[...].astype(BF)
    dwb[WROWS:, :] = jnp.zeros((WPAD - WROWS, PROJ), BF)
    for g, p, q in flat:
        src = dwb.at[pl.ds(pl.multiple_of(g * WPART, 16), WPART), :]
        send(src, r5.at[spot], S_PART, R_PART, p, q)
    myrows = pl.ds(pl.multiple_of(spot * WPART, 16), WPART)
    r5[spot] = dwb[myrows, :]
    d_pair(3)
    arrived(r5.at[pl.ds(0, PLANE - 1)], R_PART)
    tot = r5[0].astype(F32)
    for n in range(1, PLANE):
        tot = tot + r5[n].astype(F32)
    s6[...] = tot.astype(BF)
    w6[level] = s6[...]
    for p, q in pillar:
        send(s6, w6.at[level], S_LEVEL, R_LEVEL, p, q)
    merge(0)
    for n in range(3):
        arrived(r2.at[n], R_SUM + n)

    for z in range(2):
        acc = s1[0, z].astype(F32)
        for m in range(3):
            acc = acc + r2[m, z].astype(F32)
        tiles = [
            acc[:, :, s * BLOCK : (s + 1) * BLOCK].reshape(PROJ, BLOCK).T for s in range(SLOTS)
        ]
        for k in range(QBLOCKS):
            val = jnp.zeros((BLOCK, PROJ), F32)
            for s in range(SLOTS):
                hit = (kb_ref[y, s] == k) & (s < len_ref[y])
                val = val + jnp.where(hit, tiles[s], 0.0)
            dense[z * QBLOCKS + k] = val.astype(BF)

    def share(g):
        at = pl.multiple_of(lax.rem(g, 2) * TILE_ROWS, TILE_ROWS)
        return dense.at[g // 2, pl.ds(at, TILE_ROWS), :]

    r4[me] = share(me)[...]
    for g, p, q in plane:
        send(share(g), r4.at[me], S_TILE, R_TILE, p, q)
    give(3, far)
    give(3, near)
    def turn_back(w):
        arrived(back_s.at[pl.ds(0, ROWS - 1)], R_PAIR + w)
        back_s[r * COL_WIDTH + w] = dpair_s[w, rows, :]

        @pl.loop(0, ROWS)
        def _(n):
            j = n * COL_WIDTH + w
            flat_s[pl.ds(j, TILE_ROWS, stride=TILE_COLS), :] = back_s[j].astype(F32)

    stay = []
    for w in range(3):
        turn_back(w)
    arrived(w6.at[pl.ds(0, PILLAR - 1)], R_LEVEL)
    tot = w6[0].astype(F32)
    for n in range(1, PILLAR):
        tot = tot + w6[n].astype(F32)
    wtot[...] = tot.astype(BF)
    stay.append(pltpu.make_async_copy(wtot, wsum_ref.at[myrows, :], local_sem.at[2]))
    stay[-1].start()
    for _, p, q in flat:
        send(wtot, wsum_ref.at[myrows, :], S_LAST, R_LAST, p, q)
    arrived(r4.at[pl.ds(0, PLANE - 1)], R_TILE)
    val = r4[0].astype(F32)
    for n in range(1, PLANE):
        val = val + r4[n].astype(F32)
    db_ref[...] = val.T
    turn_back(3)
    dp_ref[...] = flat_s[...].reshape(TILE_ROWS, TILE_COLS, PROJ).astype(BF)
    arrived(r5.at[pl.ds(0, PLANE - 1)], R_LAST)
    for cp in stay:
        cp.wait()
    for ref, n in (
        (got.at[pl.ds(0, PLANE - 1)], S_BIAS),
        (actt.at[pl.ds(0, 28)], S_ACT),
        (gradt.at[pl.ds(0, 28)], S_GRAD),
        (mine, S_OWN),
        (r2, S_Y),
        (r2, S_FWD),
        (r1, S_SIB),
        (r2, S_SUM),
        (r4.at[pl.ds(0, PLANE - 1)], S_TILE),
        (back_s.at[pl.ds(0, 28)], S_PAIR),
        (r5.at[pl.ds(0, PLANE - 1)], S_PART),
        (w6.at[pl.ds(0, PILLAR - 1)], S_LEVEL),
        (r5.at[pl.ds(0, PLANE - 1)], S_LAST),
    ):
        settle(ref, send_sem.at[n])


def fused(key_blocks, list_len, act, grad, bias, *weights):
    any_ = pl.BlockSpec(memory_space=pl.ANY)
    smem = pl.BlockSpec(memory_space=pltpu.SMEM)
    vmem = pl.BlockSpec(memory_space=pltpu.VMEM)
    dma = pltpu.SemaphoreType.DMA
    flip = (TILE_COLS, TILE_ROWS, PROJ)
    cols = (COL_WIDTH, TOKENS, PROJ)
    tiles = (COL_WIDTH, QBLOCKS, PROJ, BLOCK)
    slots = (COL_WIDTH, QBLOCKS, SLOTS, PROJ, BLOCK)
    whole = (QBLOCKS, HEADS, BLOCK, WIDE)
    piece = (HEADS, TILE_COLS, WIDE)
    return pl.pallas_call(
        fused_kernel,
        out_shape=(
            jax.ShapeDtypeStruct((TILE_ROWS, TILE_COLS, PROJ), BF),
            jax.ShapeDtypeStruct((PROJ, TILE_ROWS), F32),
            jax.ShapeDtypeStruct((WPAD, PROJ), BF),
        ),
        in_specs=[smem] * 2 + [any_] * 2 + [vmem] * 6,
        out_specs=(vmem, vmem, any_),
        scratch_shapes=[
            pltpu.VMEM((TILE_ROWS * TILE_COLS, PROJ), F32),
            pltpu.VMEM(flip, BF), pltpu.VMEM(flip, BF),
            pltpu.VMEM(cols, BF), pltpu.VMEM(cols, BF),
            pltpu.VMEM((TILE_ROWS, PROJ), BF), pltpu.VMEM((PLANE, TILE_ROWS, PROJ), BF),
            pltpu.VMEM((2, *piece), BF), pltpu.VMEM(whole, BF),
            pltpu.VMEM((4 * PROJ, PROJ), BF),
            pltpu.VMEM((COL_WIDTH, QBLOCKS, PROJ, HEADS * BLOCK), BF),
            pltpu.VMEM((COL_WIDTH, QBLOCKS, HEADS * BLOCK, PROJ), BF),
            pltpu.VMEM(tiles, BF), pltpu.VMEM(tiles, BF),
            pltpu.VMEM(tiles, BF), pltpu.VMEM(tiles, BF),
            pltpu.VMEM(tiles, F32), pltpu.VMEM(tiles, F32),
            pltpu.VMEM(tiles, BF), pltpu.VMEM(tiles, BF), pltpu.VMEM(tiles, BF),
            pltpu.VMEM(slots, F32), pltpu.VMEM(slots, F32),
            pltpu.VMEM((QBLOCKS, WIDE, HEADS * BLOCK), F32),
            pltpu.VMEM((QBLOCKS, WIDE, HEADS * BLOCK), F32),
            pltpu.VMEM((2 * PROJ, PROJ), F32), pltpu.VMEM((PROJ, 2 * PROJ), F32),
            pltpu.VMEM((PROJ, PROJ), F32), pltpu.VMEM((COL_WIDTH, PROJ, TOKENS), BF),
            pltpu.VMEM((COL_WIDTH, 2 * PROJ, TOKENS), BF),
            pltpu.VMEM((COL_WIDTH, TOKENS, 2 * PROJ), BF), pltpu.VMEM(cols, BF),
            pltpu.VMEM((2, TILE_ROWS, TILE_COLS, PROJ), BF), pltpu.VMEM(flip, BF),
            pltpu.VMEM((WPART, PROJ), BF), dma((3,)),
            pltpu.VMEM(whole, BF), pltpu.VMEM((QBLOCKS, 2, *piece), BF),
            pltpu.VMEM((QBLOCKS, 2, *piece), BF), pltpu.VMEM((3, 2, *piece), BF),
            pltpu.VMEM((2 * QBLOCKS, BLOCK, PROJ), BF), pltpu.VMEM((PLANE, TILE_ROWS, PROJ), BF),
            pltpu.VMEM((WPAD, PROJ), BF), pltpu.VMEM((PLANE, WPART, PROJ), BF),
            pltpu.VMEM((WPART, PROJ), BF), pltpu.VMEM((PILLAR, WPART, PROJ), BF),
            dma((N_SEND,)), dma((N_RECV,)),
        ],
        compiler_params=pltpu.CompilerParams(
            collective_id=0, has_side_effects=True, vmem_limit_bytes=60 * 1024 * 1024
        ),
        name="attend_back",
    )(key_blocks, list_len, act, grad, bias, *weights)


def on_device(
    pair_act, out_grad, tri_bias, w_query, w_key, w_value, w_gate, w_out, key_blocks, list_len
):
    bias = jnp.transpose(tri_bias, (0, 2, 1)).reshape(PROJ, TILE_ROWS)
    dp, db, ws = fused(
        key_blocks, list_len, pair_act, out_grad, bias, w_query, w_key, w_value, w_gate, w_out
    )
    d_bias = jnp.transpose(db.reshape(HEADS, TILE_COLS, TILE_ROWS), (0, 2, 1))
    return (dp, d_bias) + tuple(
        ws[n * PROJ : (n + 1) * PROJ].astype(F32) for n in range(5)
    )


def solution(mesh):
    in_specs = (
        P("row", "col", None), P("row", "col", None), P(None, "row", "col"),
        P(), P(), P(), P(), P(), P(), P(),
    )
    out_specs = (P("row", "col", None), P(None, "row", "col"), P(), P(), P(), P(), P())
    return jax.shard_map(
        on_device, mesh=mesh, in_specs=in_specs, out_specs=out_specs, check_vma=False
    )
```

time: 74.8 us -> 71.4 us (0.955)
  Pallas kernels: 70.2 us -> 66.4 us
  other arithmetic: 0.72 us -> 1.55 us
    pallas_call x1, Pallas kernels: 70.2 us -> 66.4 us  [fused(): pl.pallas_call(fused_kernel, out_shape=(jax.ShapeDtypeStruct((TILE_ROWS,...]
    convert_element_type x1, other arithmetic: 0.72 us -> 1.55 us  [on_device(): ws[n * PROJ:(n + 1) * PROJ].astype(F32)]
    unnamed x6 -> x4, local copies, waits for them, and re-layouts: 2.99 us -> 2.53 us
where the time goes in v5:
time: 71.4 us; the launch traced here: 71.1 us
  Pallas kernels  66.4 us (93%)
  local copies, waits for them, and re-layouts  2.53 us (4%)
  other arithmetic  1.55 us (2%)
    pallas_call x1, Pallas kernels, fused(): pl.pallas_call(fused_kernel, out_shape=(jax.ShapeDtypeStruct((TILE_ROWS,...  66.4 us
    unnamed x4, local copies, waits for them, and re-layouts  2.53 us
    convert_element_type x1, other arithmetic, on_device(): ws[n * PROJ:(n + 1) * PROJ].astype(F32)  1.55 us

profile of v5, /device:TPU:1, one launch (start us, length us, event | category | flops | bytes accessed | tf_op | source)
XLA Modules:
  0.0 71.1 jit_solution(17921423261381542536)
XLA Ops:
  0.6 66.4 %attend_back.1 = (bf16[64,32,128]{2,1,0:T(8,128)(2,1)}, f32[128,64]{1,0:T(8,128)}, bf16[768,128]{1,0:T(8,128)(2,1)}) custom-call(s32[4,3]{1,0:T(4,128)} %kb_ref.1, s32[4]{0:T(128)} %len_ref.1, bf16[64,32,128]{2,1,0:T(8,128)(2,1)} %pair_ref.1, bf16[64,32,128]{2,1,0:T(8,128)(2,1)} %cot_ref.1, bf16[128,64]{1,0:T(8,128)(2,1)} %bitcast.7, ...), custom_call_target="tpu_custom_call" | custom-call | tf_op jit(solution)/shard_map/attend_back/pallas_call | solution.py:519
  67.0 1.5 %slice_convert_fusion = (f32[128,128]{1,0:T(8,128)}, f32[128,128]{1,0:T(8,128)}, f32[128,128]{1,0:T(8,128)}, f32[128,128]{1,0:T(8,128)}, f32[128,128]{1,0:T(8,128)}) fusion(bf16[768,128]{1,0:T(8,128)(2,1)} %get-tuple-element.12), kind=kLoop, calls=%fused_computation | loop fusion | flops 81920 | bytes 491520 | tf_op jit(solution)/shard_map/convert_element_type | solution.py:573
  68.6 0.0 copy-start
  68.6 1.9 %copy.19 = bf16[64,32,128]{2,1,0:T(8,128)(2,1)} copy(bf16[64,32,128]{2,1,0:T(8,128)(2,1)} %get-tuple-element.25) | data formatting | bytes 1048576
  70.5 0.0 copy-done
  70.5 0.6 copy.20
Async XLA Ops:
  68.6 1.9 %copy-start = (f32[128,64]{1,0:T(8,128)S(1)}, f32[128,64]{1,0:T(8,128)}, u32[]{:S(2)}) copy-start(f32[128,64]{1,0:T(8,128)} %get-tuple-element.11) | copy-start | bytes 98308

commit v6 on v5

--- a/solution.py
+++ b/solution.py
@@ -181,7 +181,8 @@
 (R_BIAS, R_ACT, R_GRAD, R_OWN, R_Y, R_FWD, R_SIB, R_SUM, R_TILE, R_PAIR, R_PART, R_LEVEL, R_LAST) = (
     0, 1, 5, 9, 10, 13, 16, 20, 23, 24, 28, 29, 30,
 )
-N_SEND, N_RECV = 13, 31
+R_FAR = 31
+N_SEND, N_RECV = 13, 32
 
 
 def settle(ref, sem):
@@ -191,7 +192,7 @@
 def fused_kernel(
     kb_ref, len_ref, pair_ref, cot_ref, bias_ref, wq_ref, wk_ref, wv_ref, wg_ref, wo_ref,
     dp_ref, db_ref, wsum_ref,
-    flat_s, actt, gradt, act_s, grad_s, turned, got, mine, full,
+    flat_s, actt, gradt, act_s, grad_s, turned, near_s, far_s, mine, full,
     wt_s, q4_s, qn_s, kt_s, vt_s, k_s, v_s, gt_s, dgt_s, dqt_s, dgp_s, gated_s, dk_s, dv_s,
     bias_s, dacc_s, dw_s, dwkv_s, dwo_s, xt_s, ga_s, gb_s, dpair_s, raw, back_s, wtot, local_sem,
     part, r1, s1, r2, dense, r4, dwb, r5, s6, w6,
@@ -243,11 +244,12 @@
                 j = m * 4 + u
                 dst[j] = flat_s[pl.ds(j, TILE_ROWS, stride=TILE_COLS), :].astype(BF)
 
-    got[me] = turned[...]
+    near_s[r] = turned[...]
     pl.semaphore_wait(barrier, len(peers))
 
-    for _, p, q in plane:
-        send(turned, got.at[me], S_BIAS, R_BIAS, p, q)
+    for n, (_, p, q) in enumerate(plane):
+        dst, ri = (near_s, R_BIAS) if n < ROWS - 1 else (far_s, R_FAR)
+        send(turned, dst.at[r], S_BIAS, ri, p, q)
     rows = pl.ds(pl.multiple_of(r * TILE_ROWS, TILE_ROWS), TILE_ROWS)
     def spread(w, offs):
         for off in offs:
@@ -271,31 +273,29 @@
     dwo_s[...] = jnp.zeros_like(dwo_s)
     dacc_s[...] = jnp.zeros_like(dacc_s)
 
-    arrived(got.at[pl.ds(0, PLANE - 1)], R_BIAS)
-    for z in range(2):
+    def piece(ref, cc):
+        at = pl.multiple_of(lax.rem(cc, 4) * TILE_COLS, TILE_COLS)
+        return ref.at[cc // 4, :, pl.ds(at, TILE_COLS), :]
+
+    sib = col_peer(c, (0, 0, 1))
+    ys = [col_peer(c, (n + 1, 0, 0)) for n in range(3)]
+
+    def layer(cc, z):
+        return cc // 4 * 4 + z * 2 + core
+
+    for first in range(2):
+        z, got = (1 - zh, far_s) if first else (zh, near_s)
+        arrived(got.at[pl.ds(0, ROWS - 1 + first)], R_FAR if first else R_BIAS)
         for s in range(SLOTS):
-            k = z * 8 + 2 * kb_ref[y, s]
+            k = 2 * kb_ref[y, s]
             tile = jnp.concatenate([got[k], got[k + 1]], axis=0).astype(F32)
             tile = jnp.where(s < len_ref[y], tile, DEAD).T.astype(BF)
             mine[z, :, :, s * BLOCK : (s + 1) * BLOCK] = tile.reshape(HEADS, TILE_COLS, BLOCK)
-
-    def piece(ref, cc):
-        at = pl.multiple_of(lax.rem(cc, 4) * TILE_COLS, TILE_COLS)
-        return ref.at[cc // 4, :, pl.ds(at, TILE_COLS), :]
-
-    sib = col_peer(c, (0, 0, 1))
-    ys = [col_peer(c, (n + 1, 0, 0)) for n in range(3)]
-
-    def layer(cc, z):
-        return cc // 4 * 4 + z * 2 + core
-
-    for z in range(2):
         send(mine.at[z], piece(full, layer(c, z)), S_OWN, R_OWN, r, sib)
-    for n in (1, 0, 2):
-        for z in range(2):
+        for n in (1, 0, 2):
             send(mine.at[z], piece(full, layer(c, z)), S_Y, R_Y + n, r, ys[n])
-    for z in range(2):
         piece(full, layer(c, z))[...] = mine[z]
+
     def column(w):
         most = pl.ds(0, TOKENS - TILE_ROWS)
         arrived(act_s.at[w, most, :], R_ACT + w)
@@ -403,11 +403,7 @@
     merge_and_send(last)
     pairs(0, 2, 3)
     gather_grads(2, 3)
-    d_pair(2)
-    give(2, far)
-    give(2, near)
     pairs(0, 3, COL_WIDTH)
-    close_block(0)
     gather_grads(3, COL_WIDTH)
     dwb[:PROJ, :] = dw_s[:PROJ, :].T.astype(BF)
     dwb[PROJ : 2 * PROJ, :] = dwkv_s[:, :PROJ].astype(BF)
@@ -420,7 +416,11 @@
         send(src, r5.at[spot], S_PART, R_PART, p, q)
     myrows = pl.ds(pl.multiple_of(spot * WPART, 16), WPART)
     r5[spot] = dwb[myrows, :]
-    d_pair(3)
+    close_block(0)
+    for w in range(2, COL_WIDTH):
+        d_pair(w)
+        give(w, far)
+        give(w, near)
     arrived(r5.at[pl.ds(0, PLANE - 1)], R_PART)
     tot = r5[0].astype(F32)
     for n in range(1, PLANE):
@@ -454,8 +454,6 @@
     r4[me] = share(me)[...]
     for g, p, q in plane:
         send(share(g), r4.at[me], S_TILE, R_TILE, p, q)
-    give(3, far)
-    give(3, near)
     def turn_back(w):
         arrived(back_s.at[pl.ds(0, ROWS - 1)], R_PAIR + w)
         back_s[r * COL_WIDTH + w] = dpair_s[w, rows, :]
@@ -488,7 +486,7 @@
     for cp in stay:
         cp.wait()
     for ref, n in (
-        (got.at[pl.ds(0, PLANE - 1)], S_BIAS),
+        (r4.at[pl.ds(0, PLANE - 1)], S_BIAS),
         (actt.at[pl.ds(0, 28)], S_ACT),
         (gradt.at[pl.ds(0, 28)], S_GRAD),
         (mine, S_OWN),
@@ -529,8 +527,8 @@
             pltpu.VMEM((TILE_ROWS * TILE_COLS, PROJ), F32),
             pltpu.VMEM(flip, BF), pltpu.VMEM(flip, BF),
             pltpu.VMEM(cols, BF), pltpu.VMEM(cols, BF),
-            pltpu.VMEM((TILE_ROWS, PROJ), BF), pltpu.VMEM((PLANE, TILE_ROWS, PROJ), BF),
-            pltpu.VMEM((2, *piece), BF), pltpu.VMEM(whole, BF),
+            pltpu.VMEM((TILE_ROWS, PROJ), BF), pltpu.VMEM((ROWS, TILE_ROWS, PROJ), BF),
+            pltpu.VMEM((ROWS, TILE_ROWS, PROJ), BF), pltpu.VMEM((2, *piece), BF), pltpu.VMEM(whole, BF),
             pltpu.VMEM((4 * PROJ, PROJ), BF),
             pltpu.VMEM((COL_WIDTH, QBLOCKS, PROJ, HEADS * BLOCK), BF),
             pltpu.VMEM((COL_WIDTH, QBLOCKS, HEADS * BLOCK, PROJ), BF),
@@ -561,17 +559,65 @@
     )(key_blocks, list_len, act, grad, bias, *weights)
 
 
+CHUNKS = 4
+
+
+def finish_kernel(dp_ref, db_ref, ws_ref, *refs):
+    pair_ref, bias_ref, w_refs = refs[0], refs[1], refs[2:7]
+    pair_s, bias_s, ws_s, w_s, get, put = refs[7:]
+    size = TILE_ROWS // CHUNKS
+    cuts = [pl.ds(n * size, size) for n in range(CHUNKS)]
+    moves = [(ws_ref, ws_s), (db_ref, bias_s)]
+    moves += [(dp_ref.at[cut], pair_s.at[cut]) for cut in cuts]
+    loads = [pltpu.make_async_copy(a, b, get.at[n]) for n, (a, b) in enumerate(moves)]
+    for cp in loads:
+        cp.start()
+    outs = [(bias_s, bias_ref)] + [(pair_s.at[cut], pair_ref.at[cut]) for cut in cuts]
+    outs += [(w_s.at[n], ref) for n, ref in enumerate(w_refs)]
+    stores = [pltpu.make_async_copy(a, b, put.at[n]) for n, (a, b) in enumerate(outs)]
+    for n in range(1 + CHUNKS):
+        loads[1 + n].wait()
+        stores[n].start()
+    loads[0].wait()
+    for n in range(5):
+        w_s[n] = ws_s[n * PROJ : (n + 1) * PROJ, :].astype(F32)
+        stores[1 + CHUNKS + n].start()
+    for cp in stores:
+        cp.wait()
+
+
+def finish(dp, db, ws):
+    any_ = pl.BlockSpec(memory_space=pl.ANY)
+    dma = pltpu.SemaphoreType.DMA
+    return pl.pallas_call(
+        finish_kernel,
+        out_shape=(
+            jax.ShapeDtypeStruct(dp.shape, BF),
+            jax.ShapeDtypeStruct(db.shape, F32),
+        )
+        + (jax.ShapeDtypeStruct((PROJ, PROJ), F32),) * 5,
+        in_specs=[any_] * 3,
+        out_specs=(any_,) * 7,
+        scratch_shapes=[
+            pltpu.VMEM(dp.shape, BF), pltpu.VMEM(db.shape, F32), pltpu.VMEM(ws.shape, BF),
+            pltpu.VMEM((5, PROJ, PROJ), F32), dma((2 + CHUNKS,)), dma((6 + CHUNKS,)),
+        ],
+        compiler_params=pltpu.CompilerParams(vmem_limit_bytes=60 * 1024 * 1024),
+        name="finish",
+    )(dp, db, ws)
+
+
 def on_device(
     pair_act, out_grad, tri_bias, w_query, w_key, w_value, w_gate, w_out, key_blocks, list_len
 ):
     bias = jnp.transpose(tri_bias, (0, 2, 1)).reshape(PROJ, TILE_ROWS)
-    dp, db, ws = fused(
-        key_blocks, list_len, pair_act, out_grad, bias, w_query, w_key, w_value, w_gate, w_out
+    d_pair, db, *d_w = finish(
+        *fused(
+            key_blocks, list_len, pair_act, out_grad, bias, w_query, w_key, w_value, w_gate, w_out
+        )
     )
     d_bias = jnp.transpose(db.reshape(HEADS, TILE_COLS, TILE_ROWS), (0, 2, 1))
-    return (dp, d_bias) + tuple(
-        ws[n * PROJ : (n + 1) * PROJ].astype(F32) for n in range(5)
-    )
+    return (d_pair, d_bias, *d_w)
 
 
 def solution(mesh):

time: 71.4 us -> 67.3 us (0.943)
  local copies, waits for them, and re-layouts: 2.53 us -> 0 us
  other arithmetic: 1.55 us -> 0 us
    unnamed x4 -> x0, local copies, waits for them, and re-layouts: 2.53 us -> none
    pallas_call x1, Pallas kernels: 66.4 us -> 64.2 us  [fused(): pl.pallas_call(fused_kernel, out_shape=(jax.ShapeDtypeStruct((TILE_ROWS,...]
    pallas_call x0 -> x1, Pallas kernels: none -> 2.11 us  [finish(): pl.pallas_call(finish_kernel, out_shape=(jax.ShapeDtypeStruct(dp.shape, B...]
    convert_element_type x1 -> x0, other arithmetic: 1.55 us -> none  [on_device(): ws[n * PROJ:(n + 1) * PROJ].astype(F32)]
where the time goes in v6:
time: 67.3 us; the launch traced here: 67.1 us
  Pallas kernels  66.3 us (99%)
  between operations  0.8 us (1%)
    pallas_call x1, Pallas kernels, fused(): pl.pallas_call(fused_kernel, out_shape=(jax.ShapeDtypeStruct((TILE_ROWS,...  64.2 us
    pallas_call x1, Pallas kernels, finish(): pl.pallas_call(finish_kernel, out_shape=(jax.ShapeDtypeStruct(dp.shape, B...  2.11 us

profile of v6, /device:TPU:1, one launch (start us, length us, event | category | flops | bytes accessed | tf_op | source)
XLA Modules:
  0.0 67.1 jit_solution(2785559971118699659)
XLA Ops:
  0.6 64.2 %attend_back.1 = (bf16[64,32,128]{2,1,0:T(8,128)(2,1)}, f32[128,64]{1,0:T(8,128)}, bf16[768,128]{1,0:T(8,128)(2,1)}) custom-call(s32[4,3]{1,0:T(4,128)} %kb_ref.1, s32[4]{0:T(128)} %len_ref.1, bf16[64,32,128]{2,1,0:T(8,128)(2,1)} %pair_ref.1, bf16[64,32,128]{2,1,0:T(8,128)(2,1)} %cot_ref.1, bf16[128,64]{1,0:T(8,128)(2,1)} %bitcast.6, ...), custom_call_target="tpu_custom_call" | custom-call | tf_op jit(solution)/shard_map/attend_back/pallas_call | solution.py:517
  64.8 2.1 %finish.1 = (bf16[64,32,128]{2,1,0:T(8,128)(2,1)}, f32[128,64]{1,0:T(8,128)}, f32[128,128]{1,0:T(8,128)}, f32[128,128]{1,0:T(8,128)}, f32[128,128]{1,0:T(8,128)}...) custom-call(bf16[64,32,128]{2,1,0:T(8,128)(2,1)} %get-tuple-element.17.dp_ref, f32[128,64]{1,0:T(8,128)} %get-tuple-element.18.db_ref, ...), custom_call_target="tpu_custom_call" | custom-call | tf_op jit(solution)/shard_map/finish/pallas_call | solution.py:592
